TPU v7x, 128 devices: a whole 4x4x4 slice. The times are simulated.
128 devices in a mesh: grp: 16 (over x, y_lo, core), blk: 8 (over z, y_hi).
Axes of the slice: x: 4, y: 4 (y_hi: 2, y_lo: 2; y = y_hi * 2 + y_lo), z: 4, core: 2. Of those that a mesh axis runs over, the one named last changes fastest.
Arguments:
- nodes: float32 [16, 3, 128, 256], P('grp', None, 'blk'), may hold values from -4 to 4
- panels: float32 [16, 3, 4096], P('grp', None, 'blk'), may hold values from -4 to 4
- nu_field: float32 [16, 128, 256], P('grp', 'blk'), may hold values from 0.2 to 1.5
- vorticity: float32 [16, 128, 256], P('grp', 'blk'), may hold values from 1 to 100
- flow: float32 [16, 4, 128, 256], P('grp', None, 'blk'), may hold values from -6 to 6
- fringe_block: int32 [16384], P(('grp', 'blk')), may hold values from 0 to 31
- fringe_size: int32 [16384], P(('grp', 'blk')), may hold values from 1 to 128
- fringe_owner: int32 [16384, 1], P(('grp', 'blk')), may hold values from 0 to 127; in each aligned block of 128 rows (0 to 127, 128 to 255, ...) at most 2 rows name the same one
- fringe_cell: int32 [16384], P(('grp', 'blk')), may hold values from 0 to 15
Outputs:
- wall_distance: float32 [16, 128, 256], P('grp', 'blk')
- nu_next: float32 [16, 128, 256], P('grp', 'blk')
- offbody: float32 [2048, 5, 128], P(('grp', 'blk'))
Inputs may be any that keep to these rules, and one draw needn't show every extreme that they name: `fringe_owner`: among the 128 slots of one device, at most 2 name the same owner device.
All inputs are finite; a program needn't handle non-finite values.
Results may differ from a plain program's by a relative error of at most 0.00012.
Values sent between devices are 32-bit elements; how exact they have to be, the bound alone decides.
No kernel may reach another device: no remote copies, remote signals or barrier semaphores. Data moves between devices by JAX's collectives and lax.ppermute only.
A program may use at most 64 MiB of HBM per device.

v0:
```python
import math

import jax
import jax.numpy as jnp
from jax import lax
from jax.sharding import PartitionSpec as P

BLOCK = 128
VARS = 5
CAP = 2
OB = 16


def padded_2(cells, sides, width):
    for axis, dim in sides:
        count = lax.axis_size(axis)
        head = lax.slice_in_dim(cells, 0, width, axis=dim)
        tail = lax.slice_in_dim(cells, cells.shape[dim] - width, cells.shape[dim], axis=dim)
        cells = jnp.concatenate(
            [
                lax.ppermute(tail, axis, [(i, (i + 1) % count) for i in range(count)]),
                cells,
                lax.ppermute(head, axis, [((i + 1) % count, i) for i in range(count)]),
            ],
            axis=dim,
        )
    return cells


def sa_step(nu_ext, dist, vort):
    centre = nu_ext[1:-1]
    east = nu_ext[2:]
    west = nu_ext[:-2]
    padded = jnp.pad(centre, ((0, 0), (1, 1)))
    north = padded[:, 2:]
    south = padded[:, :-2]
    flux = (1.0 + 0.5 * (centre + east)) * (east - centre) - (1.0 + 0.5 * (centre + west)) * (
        centre - west
    )
    flux = (
        flux
        + (1.0 + 0.5 * (centre + north)) * (north - centre)
        - (1.0 + 0.5 * (centre + south)) * (centre - south)
    )
    grads = 0.25 * ((east - west) * (east - west) + (north - south) * (north - south))
    diffusion = (flux + 0.622 * grads) / (2.0 / 3.0)
    ratio = centre / dist
    return centre + 0.02 * (0.1355 * vort * centre - 3.24 * ratio * ratio + diffusion)


def per_device(
    nodes, panels, nu_field, vorticity, flow, fringe_block, fringe_size, fringe_owner, fringe_cell
):
    lines = nodes.shape[2]
    points_j = nodes.shape[3]
    points = nodes[0].reshape(3, -1)
    init = jnp.full((points.shape[1],), 1e30, jnp.float32)
    piece = lax.all_gather(panels[0], "blk", axis=1, tiled=True)
    count = piece.shape[1]
    width = math.gcd(count, 256)
    blocks = jnp.transpose(piece.reshape(3, count // width, width), (1, 0, 2))

    def visit(carry, panel_block):
        delta0 = points[0][:, None] - panel_block[0][None, :]
        delta1 = points[1][:, None] - panel_block[1][None, :]
        delta2 = points[2][:, None] - panel_block[2][None, :]
        dsq = delta0 * delta0 + delta1 * delta1 + delta2 * delta2
        return (jnp.minimum(carry, jnp.min(dsq, axis=1)), None)

    result, unused = lax.scan(visit, init, blocks)
    dist = jnp.sqrt(result + 0.25).reshape(lines, points_j)
    vort = vorticity[0]
    nu_now = nu_field[0]
    for step in range(2):
        ext = padded_2(nu_now, (("blk", 0),), 1)
        nu_now = sa_step(ext, dist, vort)
    state = jnp.concatenate([nu_now[None], flow[0]], axis=0)
    state = state.reshape(VARS, lines * (points_j // BLOCK), BLOCK)
    values = jnp.transpose(jnp.take(state, fringe_block, axis=1), (1, 0, 2))
    live = (jnp.arange(BLOCK, dtype=jnp.int32)[None, :] < fringe_size[:, None]).astype(jnp.float32)
    values = values * live[:, None, :]
    group_count = lax.axis_size("grp")
    member_count = lax.axis_size("blk")
    devices_all = group_count * member_count
    dest = fringe_owner[:, 0]
    hits = (dest[:, None] == jnp.arange(devices_all, dtype=jnp.int32)[None, :]).astype(jnp.int32)
    rank = jnp.sum((jnp.cumsum(hits, axis=0) - hits) * hits, axis=1)
    slot = dest * CAP + rank
    buffer = jnp.zeros((devices_all * CAP, VARS, BLOCK), jnp.float32).at[slot].set(values)
    cells = (
        jnp.zeros((devices_all * CAP,), jnp.float32).at[slot].set(fringe_cell.astype(jnp.float32))
    )
    got_values, got_cells = (
        lax.all_to_all(
            buffer.reshape(devices_all, CAP, VARS, BLOCK),
            ("grp", "blk"),
            split_axis=0,
            concat_axis=0,
            tiled=True,
        ),
        lax.all_to_all(
            cells.reshape(devices_all, CAP), ("grp", "blk"), split_axis=0, concat_axis=0, tiled=True
        ),
    )
    rows = got_values.reshape(devices_all * CAP, VARS * BLOCK)
    flat_cells = got_cells.reshape(devices_all * CAP)
    select = (flat_cells[None, :] == jnp.arange(OB, dtype=jnp.float32)[:, None]).astype(jnp.float32)
    offbody = jnp.dot(
        select, rows, precision=lax.Precision.HIGHEST, preferred_element_type=jnp.float32
    )
    return (dist[None], nu_now[None], offbody.reshape(OB, VARS, BLOCK))


def solution(mesh):
    in_specs = (
        P("grp", None, "blk", None),
        P("grp", None, "blk"),
        P("grp", "blk", None),
        P("grp", "blk", None),
        P("grp", None, "blk", None),
        P(("grp", "blk")),
        P(("grp", "blk")),
        P(("grp", "blk"), None),
        P(("grp", "blk")),
    )
    out_specs = (P("grp", "blk", None), P("grp", "blk", None), P(("grp", "blk"), None, None))
    return jax.shard_map(
        per_device, mesh=mesh, in_specs=in_specs, out_specs=out_specs, check_vma=False
    )
```

profile of v0, /device:TPU:1, one launch (start us, length us, event | category | flops | bytes accessed | tf_op | source)
XLA Modules:
  0.0 139.1 jit_solution(15647237432715452222)
XLA Ops:
  1.4 7.2 %collective-permute-start = (f32[1,256]{1,0:T(1,128)S(1)}, f32[1,256]{1,0:T(1,128)S(1)}, u32[]{:S(2)}, u32[]{:S(2)}) collective-permute-start(f32[1,256]{1,0:T(1,128)S(1)} %get-tuple-element.73), channel_id=1, source_target_pairs={{1,0},{2,1},{3,2},{4,3},{5,4},{6,5},{7,6},{0,7},{9,8},{10,9},{11,1... | collective-permute-start | bytes 3080 | tf_op jit(solution)/shard_map/ppermute | solution.py:23
  13.4 9.9 %all-to-all-start = ((f32[128,1,2]{2,1,0:T(1,128)}), f32[128,1,2]{2,1,0:T(1,128)S(1)}, u32[]{:S(2)}, u32[]{:S(2)}) async-start(f32[128,1,2]{2,1,0:T(1,128)} %bitcast.9), calls=%async_computation | async-start | bytes 131072 | tf_op jit(solution)/shard_map/all_to_all | solution.py:101
  23.3 26.8 %all-gather = f32[1,3,4096]{2,0,1:T(1,128)S(1)} all-gather(f32[1,3,512]{2,0,1:T(1,128)} %param.12), channel_id=2, replica_groups=mesh['grp'=16,'blk'=8] {'blk'}, dimensions={2}, use_global_device_ids=true | all-gather | bytes 55296 | tf_op jit(solution)/shard_map/all_gather | solution.py:58
  51.1 43.5 %while.11 = (s32[]{:T(128)}, f32[4096]{0:T(1024)S(1)}, f32[3,4096]{1,0:T(4,128)S(1)}, f32[16,3,256]{2,0,1:T(8,128)S(1)}, s32[]{:T(128)}, /*index=5*/s32[]{:T(128)}, s32[]{}, s32[]{}) while((s32[]{:T(128)}, f32[4096]{0:T(1024)S(1)}, f32[3,4096]{1,0:T(4,128)S(1)}, f32[16,3,256]{2,0,1:T(8,128)S(1)}, s32[]{:T(128)}, ...), condition=%wide.region_2.3_spmd.clone, body=%wide.region_0.2_spmd.clone.sunk | while | flops 9441285 | bytes 222339 | solution.py:70
  51.2 2.6 %add_reduce_fusion.2 = f32[4096]{0:T(1024)S(1)} fusion(f32[256]{0:T(256)S(1)} %bitcast.82, f32[4096]{0:T(1024)S(1)} %bitcast.76, f32[256]{0:T(256)S(1)} %bitcast.81, f32[4096]{0:T(1024)S(1)} %bitcast.77, f32[256]{0:T(256)S(1)} %bitcast.80, f32[4096]{0:T(1024)S(1)} %bitcast.75), kind=kLoop, calls=%fused_computation.3.clone.1 | loop fusion | flops 9433088 | bytes 68608 | tf_op jit(solution)/shard_map/while/body/eval_jaxpr/reduce_min | solution.py:68
  53.9 2.6 %add_reduce_fusion.2 = f32[4096]{0:T(1024)S(1)} fusion(f32[256]{0:T(256)S(1)} %bitcast.82, f32[4096]{0:T(1024)S(1)} %bitcast.76, f32[256]{0:T(256)S(1)} %bitcast.81, f32[4096]{0:T(1024)S(1)} %bitcast.77, f32[256]{0:T(256)S(1)} %bitcast.80, f32[4096]{0:T(1024)S(1)} %bitcast.75), kind=kLoop, calls=%fused_computation.3.clone.1 | loop fusion | flops 9433088 | bytes 68608 | tf_op jit(solution)/shard_map/while/body/eval_jaxpr/reduce_min | solution.py:68
  56.7 2.6 %add_reduce_fusion.2 = f32[4096]{0:T(1024)S(1)} fusion(f32[256]{0:T(256)S(1)} %bitcast.82, f32[4096]{0:T(1024)S(1)} %bitcast.76, f32[256]{0:T(256)S(1)} %bitcast.81, f32[4096]{0:T(1024)S(1)} %bitcast.77, f32[256]{0:T(256)S(1)} %bitcast.80, f32[4096]{0:T(1024)S(1)} %bitcast.75), kind=kLoop, calls=%fused_computation.3.clone.1 | loop fusion | flops 9433088 | bytes 68608 | tf_op jit(solution)/shard_map/while/body/eval_jaxpr/reduce_min | solution.py:68
  59.4 2.6 %add_reduce_fusion.2 = f32[4096]{0:T(1024)S(1)} fusion(f32[256]{0:T(256)S(1)} %bitcast.82, f32[4096]{0:T(1024)S(1)} %bitcast.76, f32[256]{0:T(256)S(1)} %bitcast.81, f32[4096]{0:T(1024)S(1)} %bitcast.77, f32[256]{0:T(256)S(1)} %bitcast.80, f32[4096]{0:T(1024)S(1)} %bitcast.75), kind=kLoop, calls=%fused_computation.3.clone.1 | loop fusion | flops 9433088 | bytes 68608 | tf_op jit(solution)/shard_map/while/body/eval_jaxpr/reduce_min | solution.py:68
  62.1 2.6 %add_reduce_fusion.2 = f32[4096]{0:T(1024)S(1)} fusion(f32[256]{0:T(256)S(1)} %bitcast.82, f32[4096]{0:T(1024)S(1)} %bitcast.76, f32[256]{0:T(256)S(1)} %bitcast.81, f32[4096]{0:T(1024)S(1)} %bitcast.77, f32[256]{0:T(256)S(1)} %bitcast.80, f32[4096]{0:T(1024)S(1)} %bitcast.75), kind=kLoop, calls=%fused_computation.3.clone.1 | loop fusion | flops 9433088 | bytes 68608 | tf_op jit(solution)/shard_map/while/body/eval_jaxpr/reduce_min | solution.py:68
  64.8 2.6 %add_reduce_fusion.2 = f32[4096]{0:T(1024)S(1)} fusion(f32[256]{0:T(256)S(1)} %bitcast.82, f32[4096]{0:T(1024)S(1)} %bitcast.76, f32[256]{0:T(256)S(1)} %bitcast.81, f32[4096]{0:T(1024)S(1)} %bitcast.77, f32[256]{0:T(256)S(1)} %bitcast.80, f32[4096]{0:T(1024)S(1)} %bitcast.75), kind=kLoop, calls=%fused_computation.3.clone.1 | loop fusion | flops 9433088 | bytes 68608 | tf_op jit(solution)/shard_map/while/body/eval_jaxpr/reduce_min | solution.py:68
  67.5 2.6 %add_reduce_fusion.2 = f32[4096]{0:T(1024)S(1)} fusion(f32[256]{0:T(256)S(1)} %bitcast.82, f32[4096]{0:T(1024)S(1)} %bitcast.76, f32[256]{0:T(256)S(1)} %bitcast.81, f32[4096]{0:T(1024)S(1)} %bitcast.77, f32[256]{0:T(256)S(1)} %bitcast.80, f32[4096]{0:T(1024)S(1)} %bitcast.75), kind=kLoop, calls=%fused_computation.3.clone.1 | loop fusion | flops 9433088 | bytes 68608 | tf_op jit(solution)/shard_map/while/body/eval_jaxpr/reduce_min | solution.py:68
  70.3 2.6 %add_reduce_fusion.2 = f32[4096]{0:T(1024)S(1)} fusion(f32[256]{0:T(256)S(1)} %bitcast.82, f32[4096]{0:T(1024)S(1)} %bitcast.76, f32[256]{0:T(256)S(1)} %bitcast.81, f32[4096]{0:T(1024)S(1)} %bitcast.77, f32[256]{0:T(256)S(1)} %bitcast.80, f32[4096]{0:T(1024)S(1)} %bitcast.75), kind=kLoop, calls=%fused_computation.3.clone.1 | loop fusion | flops 9433088 | bytes 68608 | tf_op jit(solution)/shard_map/while/body/eval_jaxpr/reduce_min | solution.py:68
  73.0 2.6 %add_reduce_fusion.2 = f32[4096]{0:T(1024)S(1)} fusion(f32[256]{0:T(256)S(1)} %bitcast.82, f32[4096]{0:T(1024)S(1)} %bitcast.76, f32[256]{0:T(256)S(1)} %bitcast.81, f32[4096]{0:T(1024)S(1)} %bitcast.77, f32[256]{0:T(256)S(1)} %bitcast.80, f32[4096]{0:T(1024)S(1)} %bitcast.75), kind=kLoop, calls=%fused_computation.3.clone.1 | loop fusion | flops 9433088 | bytes 68608 | tf_op jit(solution)/shard_map/while/body/eval_jaxpr/reduce_min | solution.py:68
  75.7 2.6 %add_reduce_fusion.2 = f32[4096]{0:T(1024)S(1)} fusion(f32[256]{0:T(256)S(1)} %bitcast.82, f32[4096]{0:T(1024)S(1)} %bitcast.76, f32[256]{0:T(256)S(1)} %bitcast.81, f32[4096]{0:T(1024)S(1)} %bitcast.77, f32[256]{0:T(256)S(1)} %bitcast.80, f32[4096]{0:T(1024)S(1)} %bitcast.75), kind=kLoop, calls=%fused_computation.3.clone.1 | loop fusion | flops 9433088 | bytes 68608 | tf_op jit(solution)/shard_map/while/body/eval_jaxpr/reduce_min | solution.py:68
  78.4 2.6 %add_reduce_fusion.2 = f32[4096]{0:T(1024)S(1)} fusion(f32[256]{0:T(256)S(1)} %bitcast.82, f32[4096]{0:T(1024)S(1)} %bitcast.76, f32[256]{0:T(256)S(1)} %bitcast.81, f32[4096]{0:T(1024)S(1)} %bitcast.77, f32[256]{0:T(256)S(1)} %bitcast.80, f32[4096]{0:T(1024)S(1)} %bitcast.75), kind=kLoop, calls=%fused_computation.3.clone.1 | loop fusion | flops 9433088 | bytes 68608 | tf_op jit(solution)/shard_map/while/body/eval_jaxpr/reduce_min | solution.py:68
  81.1 2.6 %add_reduce_fusion.2 = f32[4096]{0:T(1024)S(1)} fusion(f32[256]{0:T(256)S(1)} %bitcast.82, f32[4096]{0:T(1024)S(1)} %bitcast.76, f32[256]{0:T(256)S(1)} %bitcast.81, f32[4096]{0:T(1024)S(1)} %bitcast.77, f32[256]{0:T(256)S(1)} %bitcast.80, f32[4096]{0:T(1024)S(1)} %bitcast.75), kind=kLoop, calls=%fused_computation.3.clone.1 | loop fusion | flops 9433088 | bytes 68608 | tf_op jit(solution)/shard_map/while/body/eval_jaxpr/reduce_min | solution.py:68
  83.9 2.6 %add_reduce_fusion.2 = f32[4096]{0:T(1024)S(1)} fusion(f32[256]{0:T(256)S(1)} %bitcast.82, f32[4096]{0:T(1024)S(1)} %bitcast.76, f32[256]{0:T(256)S(1)} %bitcast.81, f32[4096]{0:T(1024)S(1)} %bitcast.77, f32[256]{0:T(256)S(1)} %bitcast.80, f32[4096]{0:T(1024)S(1)} %bitcast.75), kind=kLoop, calls=%fused_computation.3.clone.1 | loop fusion | flops 9433088 | bytes 68608 | tf_op jit(solution)/shard_map/while/body/eval_jaxpr/reduce_min | solution.py:68
  86.6 2.6 %add_reduce_fusion.2 = f32[4096]{0:T(1024)S(1)} fusion(f32[256]{0:T(256)S(1)} %bitcast.82, f32[4096]{0:T(1024)S(1)} %bitcast.76, f32[256]{0:T(256)S(1)} %bitcast.81, f32[4096]{0:T(1024)S(1)} %bitcast.77, f32[256]{0:T(256)S(1)} %bitcast.80, f32[4096]{0:T(1024)S(1)} %bitcast.75), kind=kLoop, calls=%fused_computation.3.clone.1 | loop fusion | flops 9433088 | bytes 68608 | tf_op jit(solution)/shard_map/while/body/eval_jaxpr/reduce_min | solution.py:68
  89.3 2.6 %add_reduce_fusion.2 = f32[4096]{0:T(1024)S(1)} fusion(f32[256]{0:T(256)S(1)} %bitcast.82, f32[4096]{0:T(1024)S(1)} %bitcast.76, f32[256]{0:T(256)S(1)} %bitcast.81, f32[4096]{0:T(1024)S(1)} %bitcast.77, f32[256]{0:T(256)S(1)} %bitcast.80, f32[4096]{0:T(1024)S(1)} %bitcast.75), kind=kLoop, calls=%fused_computation.3.clone.1 | loop fusion | flops 9433088 | bytes 68608 | tf_op jit(solution)/shard_map/while/body/eval_jaxpr/reduce_min | solution.py:68
  95.0 3.5 %collective-permute-start.2 = (f32[1,256]{1,0:T(1,128)S(1)}, f32[1,256]{1,0:T(1,128)S(1)}, u32[]{:S(2)}, u32[]{:S(2)}) collective-permute-start(f32[1,256]{1,0:T(1,128)S(1)} %get-tuple-element.71), channel_id=1, source_target_pairs={{1,0},{2,1},{3,2},{4,3},{5,4},{6,5},{7,6},{0,7},{9,8},{10,9},{11,1... | collective-permute-start | bytes 3080 | tf_op jit(solution)/shard_map/ppermute | solution.py:23
  99.2 5.3 %collective-permute-done.3 = f32[1,256]{1,0:T(1,128)S(1)} collective-permute-done((f32[1,256]{1,0:T(1,128)S(1)}, f32[1,256]{1,0:T(1,128)S(1)}, u32[]{:S(2)}, u32[]{:S(2)}) %collective-permute-start.3) | collective-permute-done | bytes 1056 | tf_op jit(solution)/shard_map/ppermute | solution.py:21
  105.8 4.3 %scatter_fusion = f32[256,5,128]{2,1,0:T(8,128)S(1)} fusion(f32[256,5,128]{2,1,0:T(8,128)S(1)} %broadcast_in_dim.35, s32[128]{0:T(128)S(1)} %fusion.52, f32[128,5,128]{2,1,0:T(8,128)S(1)} %select_multiply_fusion), kind=kCustom, calls=%fused_computation.2 | custom fusion | bytes 983552 | tf_op jit(solution)/shard_map/scatter | solution.py:89
  111.3 10.9 %all-to-all-start.1 = ((f32[128,2,5,128]{3,1,2,0:T(2,128)}), f32[128,2,5,128]{3,1,2,0:T(2,128)S(1)}, u32[]{:S(2)}, u32[]{:S(2)}) async-start(f32[128,2,5,128]{3,1,2,0:T(2,128)} %copy.32), calls=%async_computation.1 | async-start | bytes 1310720 | tf_op jit(solution)/shard_map/all_to_all | solution.py:94
  124.3 13.3 %all-to-all-done.1 = f32[128,2,5,128]{3,1,2,0:T(2,128)S(1)} async-done(((f32[128,2,5,128]{3,1,2,0:T(2,128)}), f32[128,2,5,128]{3,1,2,0:T(2,128)S(1)}, u32[]{:S(2)}, u32[]{:S(2)}) %all-to-all-start.1) | async-done | bytes 655392 | tf_op jit(solution)/shard_map/all_to_all | solution.py:94
  (104 shorter events, 17.0 us)
Async XLA Ops:
  1.4 93.5 %collective-permute-start = (f32[1,256]{1,0:T(1,128)S(1)}, f32[1,256]{1,0:T(1,128)S(1)}, u32[]{:S(2)}, u32[]{:S(2)}) collective-permute-start(f32[1,256]{1,0:T(1,128)S(1)} %get-tuple-element.73), channel_id=1, source_target_pairs={{1,0},{2,1},{3,2},{4,3},{5,4},{6,5},{7,6},{0,7},{9,8},{10,9},{11,1... | collective-permute-start | bytes 3080 | tf_op jit(solution)/shard_map/ppermute | solution.py:23
  8.6 86.3 %collective-permute-start.1 = (f32[1,256]{1,0:T(1,128)S(1)}, f32[1,256]{1,0:T(1,128)S(1)}, u32[]{:S(2)}, u32[]{:S(2)}) collective-permute-start(f32[1,256]{1,0:T(1,128)S(1)} %get-tuple-element.74), channel_id=1, source_target_pairs={{0,1},{1,2},{2,3},{3,4},{4,5},{5,6},{6,7},{7,0},{8,9},{9,10},{10,1... | collective-permute-start | bytes 3080 | tf_op jit(solution)/shard_map/ppermute | solution.py:21
  12.6 82.1 %copy-start.5 = (s32[128]{0:T(128)S(1)}, s32[128]{0:T(128)}, u32[]{:S(2)}) copy-start(s32[128]{0:T(128)} %param.16) | copy-start | bytes 1540
  12.6 82.1 %copy-start.4 = (s32[128]{0:T(128)S(1)}, s32[128]{0:T(128)}, u32[]{:S(2)}) copy-start(s32[128]{0:T(128)} %param.17) | copy-start | bytes 1540
  13.4 81.5 %copy-start.2 = (f32[1,16,256]{2,1,0:T(8,128)S(1)}, f32[1,16,256]{2,1,0:T(8,128)}, u32[]{:S(2)}) copy-start(f32[1,16,256]{2,1,0:T(8,128)} %param.14) | copy-start | bytes 49156
  13.4 81.5 %copy-start.3 = (f32[1,16,256]{2,1,0:T(8,128)S(1)}, f32[1,16,256]{2,1,0:T(8,128)}, u32[]{:S(2)}) copy-start(f32[1,16,256]{2,1,0:T(8,128)} %param.13) | copy-start | bytes 49156
  13.4 97.9 %all-to-all-start = ((f32[128,1,2]{2,1,0:T(1,128)}), f32[128,1,2]{2,1,0:T(1,128)S(1)}, u32[]{:S(2)}, u32[]{:S(2)}) async-start(f32[128,1,2]{2,1,0:T(1,128)} %bitcast.9), calls=%async_computation | async-start | bytes 131072 | tf_op jit(solution)/shard_map/all_to_all | solution.py:101
  23.3 75.2 %copy-start = (f32[1,4,16,256]{3,2,1,0:T(8,128)S(1)}, f32[1,4,16,256]{3,2,1,0:T(8,128)}, u32[]{:S(2)}) copy-start(f32[1,4,16,256]{3,2,1,0:T(8,128)} %param.15) | copy-start | bytes 196612
  95.0 4.3 %collective-permute-start.2 = (f32[1,256]{1,0:T(1,128)S(1)}, f32[1,256]{1,0:T(1,128)S(1)}, u32[]{:S(2)}, u32[]{:S(2)}) collective-permute-start(f32[1,256]{1,0:T(1,128)S(1)} %get-tuple-element.71), channel_id=1, source_target_pairs={{1,0},{2,1},{3,2},{4,3},{5,4},{6,5},{7,6},{0,7},{9,8},{10,9},{11,1... | collective-permute-start | bytes 3080 | tf_op jit(solution)/shard_map/ppermute | solution.py:23
  98.5 6.0 %collective-permute-start.3 = (f32[1,256]{1,0:T(1,128)S(1)}, f32[1,256]{1,0:T(1,128)S(1)}, u32[]{:S(2)}, u32[]{:S(2)}) collective-permute-start(f32[1,256]{1,0:T(1,128)S(1)} %get-tuple-element.72), channel_id=1, source_target_pairs={{0,1},{1,2},{2,3},{3,4},{4,5},{5,6},{6,7},{7,0},{8,9},{9,10},{10,1... | collective-permute-start | bytes 3080 | tf_op jit(solution)/shard_map/ppermute | solution.py:21
  104.6 1.1 copy-start.1
  111.3 26.3 %all-to-all-start.1 = ((f32[128,2,5,128]{3,1,2,0:T(2,128)}), f32[128,2,5,128]{3,1,2,0:T(2,128)S(1)}, u32[]{:S(2)}, u32[]{:S(2)}) async-start(f32[128,2,5,128]{3,1,2,0:T(2,128)} %copy.32), calls=%async_computation.1 | async-start | bytes 1310720 | tf_op jit(solution)/shard_map/all_to_all | solution.py:94
where the time goes:
time: 140 us; the launch traced here: 139 us
  other arithmetic  46.4 us (33%)
  starting transfers between devices  31.6 us (23%)
  blocking collectives  26.8 us (19%)
  waiting for transfers between devices  19.3 us (14%)
  local copies, waits for them, and re-layouts  12.3 us (9%)
    reduce_min x16, other arithmetic, visit(): return (jnp.minimum(carry, jnp.min(dsq, axis=1)), None)  41.7 us
    all_gather x1, blocking collectives, per_device(): piece = lax.all_gather(panels[0], 'blk', axis=1, tiled=True)  26.8 us
    all_to_all x1, waiting for transfers between devices, per_device(): lax.all_to_all(buffer.reshape(devices_all, CAP, VARS, BLOCK), ('grp', 'bl...  13.3 us
    all_to_all x1, starting transfers between devices, per_device(): lax.all_to_all(buffer.reshape(devices_all, CAP, VARS, BLOCK), ('grp', 'bl...  10.9 us
    ppermute x2, starting transfers between devices, padded_2(): lax.ppermute(head, axis, [((i + 1) % count, i) for i in range(count)])  10.7 us
    all_to_all x1, starting transfers between devices, per_device(): lax.all_to_all(cells.reshape(devices_all, CAP), ('grp', 'blk'), split_axi...  9.92 us
    ppermute x2, waiting for transfers between devices, padded_2(): lax.ppermute(tail, axis, [(i, (i + 1) % count) for i in range(count)])  5.31 us
    scatter x1, local copies, waits for them, and re-layouts, per_device(): jnp.zeros((devices_all * CAP, VARS, BLOCK), jnp.float32).at[slot]  4.3 us
  transfers between devices with their start and end apart: 6, of which 3 were waited for; matrix products, arithmetic and copies ran while one was open for 41% of the time, Pallas kernels for 0%

commit v1 on v0

v1 whole, which is shorter than its diff:
```python
import functools

import jax
import jax.numpy as jnp
from jax import lax
from jax.experimental import pallas as pl
from jax.experimental.pallas import tpu as pltpu
from jax.sharding import PartitionSpec as P

BLOCK = 128
VARS = 5
CAP = 2
OB = 16
PEERS = 8
DEVS = 128
LINES = 16
NJ = 256
PQ = 4
PAY = 40
NU0 = 16
VO0 = 24
ND0 = 28
FR = 9
F32 = jnp.float32
BF16 = jnp.bfloat16


def iota(shape, axis):
    return lax.broadcasted_iota(jnp.int32, shape, axis)


def split3(v):
    high = v.astype(BF16)
    rest = v - high.astype(F32)
    mid = rest.astype(BF16)
    low = (rest - mid.astype(F32)).astype(BF16)
    return high, mid, low


def onehot(cond):
    return jnp.where(cond, 1.0, 0.0).astype(BF16)


def contract_lanes(a, b):
    return lax.dot_general(a, b, (((1,), (1,)), ((), ())), preferred_element_type=F32)


def halves(rows):
    return jnp.concatenate([rows[:, :BLOCK], rows[:, BLOCK:]], axis=0)


def pack_kernel(nodes_ref, panels_ref, nu_ref, vort_ref, out_ref):
    def put(row, value):
        out_ref[pl.ds(row, 1), :] = value

    p = [panels_ref[c] for c in range(3)]
    square = p[0] * p[0] + p[1] * p[1] + p[2] * p[2]
    for q in range(PQ):
        for c, vec in enumerate((p[0], p[1], p[2], square)):
            put(q * 4 + c, vec[:, q * BLOCK : (q + 1) * BLOCK])
    for half in range(2):
        lanes = slice(half * BLOCK, (half + 1) * BLOCK)
        for at, line in enumerate((0, 1, LINES - 2, LINES - 1)):
            put(NU0 + at * 2 + half, nu_ref[line : line + 1, lanes])
        for at, line in enumerate((0, LINES - 1)):
            put(VO0 + at * 2 + half, vort_ref[line : line + 1, lanes])
            for c in range(3):
                put(ND0 + c * 4 + at * 2 + half, nodes_ref[c, line : line + 1, lanes])
    block = out_ref[0:PAY, :]
    for s in range(1, PEERS):
        out_ref[s * PAY : (s + 1) * PAY, :] = block


def route_kernel(owner_ref, block_ref, size_ref, cell_ref, flow_ref, send_ref, pick_ref, live_ref):
    square = (DEVS, DEVS)
    row = iota(square, 0)
    lane = iota(square, 1)
    owner = owner_ref[...]
    hits = onehot(jnp.broadcast_to(owner, square) == row)
    before = onehot(row < lane)
    earlier = jnp.dot(hits, before, preferred_element_type=F32)
    rank = jnp.sum(hits.astype(F32) * earlier, axis=0, keepdims=True)
    slot = owner * CAP + rank.astype(jnp.int32)
    block = block_ref[...]
    place = (block % 2) * LINES + block // 2
    places = onehot((jnp.broadcast_to(place, square) == row % 32) & (row < 96))
    sizes = jnp.broadcast_to(size_ref[...], square).astype(F32).astype(BF16)
    cell = jnp.broadcast_to(cell_ref[...], square)
    state = jnp.concatenate([halves(flow_ref[v]) for v in range(VARS - 1)], axis=1)
    high, mid, low = split3(state)
    table = jnp.concatenate([high, mid, low, jnp.zeros_like(high)], axis=0)
    cells = None
    for r in range(CAP):
        sel = onehot(jnp.broadcast_to(slot, square) == row * CAP + r)
        pick = contract_lanes(sel, places)
        live = jnp.where(lane.astype(F32) < contract_lanes(sel, sizes), 1.0, 0.0)
        named = contract_lanes(sel, onehot((cell == row - r * OB) & (row < (r + 1) * OB)))
        cells = named if cells is None else cells + named
        pick_ref[pl.ds(r, DEVS, stride=CAP), :] = pick
        live_ref[pl.ds(r, DEVS, stride=CAP), :] = live
        values = jnp.dot(pick.astype(BF16), table, preferred_element_type=F32)
        for v in range(VARS - 1):
            send_ref[pl.ds(r * (VARS - 1) + v, DEVS, stride=FR), :] = (
                values[:, v * BLOCK : (v + 1) * BLOCK] * live
            )
    send_ref[pl.ds(FR - 1, DEVS, stride=FR), :] = cells


def sa_step(centre, east, west, dist, vort):
    lane = iota(centre.shape, 1)
    north = jnp.where(lane == NJ - 1, 0.0, pltpu.roll(centre, NJ - 1, 1))
    south = jnp.where(lane == 0, 0.0, pltpu.roll(centre, 1, 1))
    flux = (1.0 + 0.5 * (centre + east)) * (east - centre) - (1.0 + 0.5 * (centre + west)) * (
        centre - west
    )
    flux = (
        flux
        + (1.0 + 0.5 * (centre + north)) * (north - centre)
        - (1.0 + 0.5 * (centre + south)) * (centre - south)
    )
    grads = 0.25 * ((east - west) * (east - west) + (north - south) * (north - south))
    diffusion = (flux + 0.622 * grads) * 1.5
    ratio = centre / dist
    return centre + 0.02 * (0.1355 * vort * centre - 3.24 * ratio * ratio + diffusion)


def step_kernel(
    got_ref, nodes_ref, nu_ref, vort_ref, pick_ref, live_ref,
    dist_ref, next_ref, send_ref,
    lhs_ref, node_ext, nu_ext, vort_ext, dist_ext,
):
    me = lax.axis_index("blk")
    left = lax.rem(me + PEERS - 1, PEERS) * PAY
    right = lax.rem(me + 1, PEERS) * PAY

    def edge(base, row):
        return jnp.concatenate(
            [got_ref[pl.ds(base + row, 1), :], got_ref[pl.ds(base + row + 1, 1), :]], axis=1
        )

    for c in range(3):
        node_ext[c, 1 : 1 + LINES, :] = nodes_ref[c]
        node_ext[c, 0:1, :] = edge(left, ND0 + c * 4 + 2)
        node_ext[c, 1 + LINES : 2 + LINES, :] = edge(right, ND0 + c * 4)
    nu_ext[2 : 2 + LINES, :] = nu_ref[...]
    vort_ext[1 : 1 + LINES, :] = vort_ref[...]
    for at in range(2):
        nu_ext[at : at + 1, :] = edge(left, NU0 + 4 + at * 2)
        nu_ext[2 + LINES + at : 3 + LINES + at, :] = edge(right, NU0 + at * 2)
    vort_ext[0:1, :] = edge(left, VO0 + 2)
    vort_ext[1 + LINES : 2 + LINES, :] = edge(right, VO0)

    for s in range(PEERS):
        high, mid, low = [t.astype(F32) for t in split3(got_ref[pl.ds(s * PAY, PQ * 4), :])]
        none = jnp.zeros_like(high)
        terms = jnp.concatenate([high, high, high, mid, mid, low, none, none], axis=0)
        lhs_ref[s * BLOCK : (s + 1) * BLOCK, :] = terms.T.astype(BF16)

    c4 = iota((PQ * 4, NJ), 0) % 4
    q4 = iota((PQ * 4, NJ), 0) // 4

    def line(i, unused):
        x, y, z = [
            jnp.broadcast_to(node_ext[c, pl.ds(i, 1), :], (PQ * 4, NJ)) for c in range(3)
        ]
        square = (x * x + y * y + z * z)[0:1]
        base = jnp.where(c4 == 0, x, jnp.where(c4 == 1, y, z)) * -2.0
        base = jnp.where(c4 == 3, 1.0, base)
        best = None
        for q in range(PQ):
            high, mid, low = split3(jnp.where(q4 == q, base, 0.0))
            none = jnp.zeros_like(high)
            w = jnp.concatenate([high, mid, low, high, mid, high, none, none], axis=0)
            rest = jnp.dot(lhs_ref[...], w, preferred_element_type=F32)
            low8 = jnp.min(rest.reshape(PEERS * BLOCK // 8, 8, NJ), axis=0)
            best = low8 if best is None else jnp.minimum(best, low8)
        least = jnp.min(best, axis=0, keepdims=True) + square
        dist_ext[pl.ds(i, 1), :] = jnp.sqrt(jnp.maximum(least, 0.0) + 0.25)
        return unused

    lax.fori_loop(0, LINES + 2, line, 0)

    mid_nu = sa_step(
        nu_ext[1 : 3 + LINES, :],
        nu_ext[2 : 4 + LINES, :],
        nu_ext[0 : 2 + LINES, :],
        dist_ext[0 : 2 + LINES, :],
        vort_ext[0 : 2 + LINES, :],
    )
    nu_ext[0 : 2 + LINES, :] = mid_nu
    dist = dist_ext[1 : 1 + LINES, :]
    new = sa_step(
        nu_ext[1 : 1 + LINES, :],
        nu_ext[2 : 2 + LINES, :],
        nu_ext[0:LINES, :],
        dist,
        vort_ref[...],
    )
    dist_ref[...] = dist
    next_ref[...] = new
    high, mid, low = split3(halves(new))
    table = jnp.concatenate([high, mid, low, jnp.zeros_like(high)], axis=0)
    values = jnp.dot(pick_ref[...].astype(BF16), table, preferred_element_type=F32)
    send_ref[...] = values * live_ref[...]


def add_up(chosen, rows):
    total = None
    for part in split3(rows):
        term = jnp.dot(chosen, part, preferred_element_type=F32)
        total = term if total is None else total + term
    return total


def flow_sum_kernel(got_ref, sums_ref, chosen_ref):
    cells = got_ref[pl.ds(FR - 1, DEVS, stride=FR), :].T
    chosen = jnp.concatenate([cells[r * OB : (r + 1) * OB] for r in range(CAP)], axis=1)
    chosen_ref[...] = chosen
    chosen = chosen.astype(BF16)
    for v in range(VARS - 1):
        rows = jnp.concatenate(
            [
                got_ref[pl.ds(r * (VARS - 1) + v, DEVS, stride=FR), :]
                for r in range(CAP)
            ],
            axis=0,
        )
        sums_ref[v] = add_up(chosen, rows)


def nu_sum_kernel(got_ref, sums_ref, chosen_ref, out_ref):
    rows = jnp.concatenate(
        [got_ref[pl.ds(r, DEVS, stride=CAP), :] for r in range(CAP)], axis=0
    )
    out_ref[0] = add_up(chosen_ref[...].astype(BF16), rows)
    out_ref[1:VARS] = sums_ref[...]


def call(kernel, outs, *args, scratch=()):
    return pl.pallas_call(
        kernel,
        out_shape=tuple(jax.ShapeDtypeStruct(shape, F32) for shape in outs),
        scratch_shapes=list(scratch),
    )(*args)


def exchange(rows, count, axes):
    sent = rows.reshape(count, 1, -1)
    got = lax.all_to_all(sent, axes, split_axis=0, concat_axis=0, tiled=True)
    return got.reshape(rows.shape)


def per_device(
    nodes, panels, nu_field, vorticity, flow, fringe_block, fringe_size, fringe_owner, fringe_cell
):
    nodes, nu, vort, flow = nodes[0], nu_field[0], vorticity[0], flow[0]
    (pay,) = call(
        pack_kernel, [(PEERS * PAY, BLOCK)], nodes, panels.reshape(3, 1, PQ * BLOCK), nu, vort
    )
    pay = exchange(pay, PEERS, "blk")
    wide = (1, DEVS)
    send, pick, live = call(
        route_kernel,
        [(DEVS * FR, BLOCK), (DEVS * CAP, BLOCK), (DEVS * CAP, BLOCK)],
        fringe_owner.reshape(wide),
        fringe_block.reshape(wide),
        fringe_size.reshape(wide),
        fringe_cell.reshape(wide),
        flow,
    )
    flow_rows = exchange(send, DEVS, ("grp", "blk"))
    line = (LINES, NJ)
    ext = pltpu.VMEM((24, NJ), F32)
    dist, nu_next, send = call(
        step_kernel,
        [line, line, (DEVS * CAP, BLOCK)],
        pay, nodes, nu, vort, pick, live,
        scratch=(
            pltpu.VMEM((PEERS * BLOCK, BLOCK), BF16),
            pltpu.VMEM((3, 24, NJ), F32),
            ext, ext, ext,
        ),
    )
    nu_rows = exchange(send, DEVS, ("grp", "blk"))
    sums, chosen = call(
        flow_sum_kernel, [(VARS - 1, OB, BLOCK), (OB, CAP * DEVS)], flow_rows
    )
    (offbody,) = call(nu_sum_kernel, [(VARS, OB, BLOCK)], nu_rows, sums, chosen)
    return (dist[None], nu_next[None], jnp.transpose(offbody, (1, 0, 2)))


def solution(mesh):
    in_specs = (
        P("grp", None, "blk", None),
        P("grp", None, "blk"),
        P("grp", "blk", None),
        P("grp", "blk", None),
        P("grp", None, "blk", None),
        P(("grp", "blk")),
        P(("grp", "blk")),
        P(("grp", "blk"), None),
        P(("grp", "blk")),
    )
    out_specs = (P("grp", "blk", None), P("grp", "blk", None), P(("grp", "blk"), None, None))
    return jax.shard_map(
        per_device, mesh=mesh, in_specs=in_specs, out_specs=out_specs, check_vma=False
    )
```

time: 140 us -> 63 us (0.45)
  other arithmetic: 46.4 us -> 0 us
  blocking collectives: 26.8 us -> 0 us
  Pallas kernels: 0 us -> 22.7 us
  local copies, waits for them, and re-layouts: 12.3 us -> 1.31 us
  starting transfers between devices: 31.6 us -> 25 us
  waiting for transfers between devices: 19.3 us -> 12.9 us
    reduce_min x16 -> x0, other arithmetic: 41.7 us -> none  [visit(): return (jnp.minimum(carry, jnp.min(dsq, axis=1)), None)]
    all_gather x1 -> x0, blocking collectives: 26.8 us -> none  [per_device(): piece = lax.all_gather(panels[0], 'blk', axis=1, tiled=True)]
    pallas_call x0 -> x5, Pallas kernels: none -> 22.7 us  [call(): pl.pallas_call(kernel, out_shape=tuple((jax.ShapeDtypeStruct(shape, F32)...]
    ppermute x4 -> x0, starting transfers between devices: 10.7 us -> none  [the longest x2 10.7 us: padded_2(): lax.ppermute(head, axis, [((i + 1) % count, i) for i in range(count)])]
    ppermute x4 -> x0, waiting for transfers between devices: 5.95 us -> none  [the longest x2 5.31 us: padded_2(): lax.ppermute(tail, axis, [(i, (i + 1) % count) for i in range(count)])]
    scatter x2 -> x0, local copies, waits for them, and re-layouts: 5.28 us -> none  [the longest x1 4.3 us: per_device(): jnp.zeros((devices_all * CAP, VARS, BLOCK), jnp.float32).at[slot]]
    all_to_all x2 -> x3, starting transfers between devices: 20.8 us -> 25 us  [exchange(): got = lax.all_to_all(sent, axes, split_axis=0, concat_axis=0, tiled=True)]
    slice x34 -> x0, local copies, waits for them, and re-layouts: 1.58 us -> none  [the longest x32 0.85 us: visit(): delta0 = points[0][:, None] - panel_block[0][None, :]]
  transfers between devices with their start and end apart: 6 -> 3, of which waited for: 3 -> 2; matrix products, arithmetic and copies ran while one was open for 41% -> 0% of each run, Pallas kernels for 0% -> 31%
where the time goes in v1:
time: 63 us; the launch traced here: 62.5 us
  starting transfers between devices  25 us (40%)
  Pallas kernels  22.7 us (36%)
  waiting for transfers between devices  12.9 us (20%)
  local copies, waits for them, and re-layouts  1.31 us (2%)
  between operations  0.66 us (1%)
    all_to_all x3, starting transfers between devices, exchange(): got = lax.all_to_all(sent, axes, split_axis=0, concat_axis=0, tiled=True)  25 us
    pallas_call x5, Pallas kernels, call(): pl.pallas_call(kernel, out_shape=tuple((jax.ShapeDtypeStruct(shape, F32)...  22.7 us
    all_to_all x3, waiting for transfers between devices, exchange(): got = lax.all_to_all(sent, axes, split_axis=0, concat_axis=0, tiled=True)  12.9 us
    unnamed x6, local copies, waits for them, and re-layouts  1.31 us
  transfers between devices with their start and end apart: 3, of which 2 were waited for; matrix products, arithmetic and copies ran while one was open for 0% of the time, Pallas kernels for 31%

profile of v1, /device:TPU:1, one launch (start us, length us, event | category | flops | bytes accessed | tf_op | source)
XLA Modules:
  0.0 62.5 jit_solution(5676828757874998210)
XLA Ops:
  0.6 1.5 %shard_map.112 = f32[320,128]{1,0:T(8,128)} custom-call(f32[3,16,256]{2,1,0:T(8,128)} %bitcast.23, f32[3,1,512]{2,1,0:T(1,128)} %bitcast.32, f32[16,256]{1,0:T(8,128)} %bitcast.27, f32[16,256]{1,0:T(8,128)} %bitcast.29), custom_call_target="tpu_custom_call" | custom-call | tf_op jit(solution)/shard_map/pallas_call | solution.py:240
  2.1 8.5 %all-to-all-start = ((f32[8,1,5120]{2,1,0:T(1,128)}), f32[8,1,5120]{2,1,0:T(1,128)S(1)}, u32[]{:S(2)}, u32[]{:S(2)}) async-start(f32[8,1,5120]{2,1,0:T(1,128)} %bitcast.20), calls=%async_computation | async-start | bytes 327680 | tf_op jit(solution)/shard_map/all_to_all | solution.py:249
  10.6 2.3 %shard_map.113 = (f32[1152,128]{1,0:T(8,128)}, f32[256,128]{1,0:T(8,128)}, f32[256,128]{1,0:T(8,128)}) custom-call(s32[1,128]{1,0:T(1,128)} %bitcast.33, s32[1,128]{1,0:T(1,128)} %bitcast.34, s32[1,128]{1,0:T(1,128)} %bitcast.35, s32[1,128]{1,0:T(1,128)} %bitcast.36, f32[4,16,256]{2,1,0:T(8,128)} %bitcast.26), custom_call_target="tpu_custom_call" | custom-call | tf_op jit(solution)/shard_map/pallas_call | solution.py:240
  13.0 4.9 %all-to-all-done = f32[8,1,5120]{2,1,0:T(1,128)S(1)} async-done(((f32[8,1,5120]{2,1,0:T(1,128)}), f32[8,1,5120]{2,1,0:T(1,128)S(1)}, u32[]{:S(2)}, u32[]{:S(2)}) %all-to-all-start) | async-done | bytes 163872 | tf_op jit(solution)/shard_map/all_to_all | solution.py:249
  17.8 0.0 copy-start.1
  17.8 0.7 %copy-done.1 = f32[8,1,5120]{2,1,0:T(1,128)} copy-done((f32[8,1,5120]{2,1,0:T(1,128)}, f32[8,1,5120]{2,1,0:T(1,128)S(1)}, u32[]{:S(2)}) %copy-start.1) | copy-done | bytes 163864
  18.5 6.8 %all-to-all-start.2 = ((f32[128,1,1152]{2,1,0:T(1,128)}), f32[128,1,1152]{2,1,0:T(1,128)S(1)}, u32[]{:S(2)}, u32[]{:S(2)}) async-start(f32[128,1,1152]{2,1,0:T(1,128)} %bitcast.21), calls=%async_computation.2 | async-start | bytes 1179648 | tf_op jit(solution)/shard_map/all_to_all | solution.py:249
  25.3 15.2 %shard_map.114 = (f32[16,256]{1,0:T(8,128)}, f32[16,256]{1,0:T(8,128)}, f32[256,128]{1,0:T(8,128)}) custom-call(f32[320,128]{1,0:T(8,128)} %bitcast.19, f32[3,16,256]{2,1,0:T(8,128)} %bitcast.24, f32[16,256]{1,0:T(8,128)} %bitcast.28, f32[16,256]{1,0:T(8,128)} %bitcast.30, f32[256,128]{1,0:T(8,128)} %get-tuple-element.11.pick_ref, ...), custom_call_target="tpu_custom_call" | custom-call | tf_op jit(solution)/shard_map/pallas_call | solution.py:240
  40.5 0.0 all-to-all-done.2
  40.5 0.0 copy-start
  40.5 9.7 %all-to-all-start.1 = ((f32[128,1,256]{2,1,0:T(1,128)}), f32[128,1,256]{2,1,0:T(1,128)S(1)}, u32[]{:S(2)}, u32[]{:S(2)}) async-start(f32[128,1,256]{2,1,0:T(1,128)} %bitcast.25), calls=%async_computation.1 | async-start | bytes 262144 | tf_op jit(solution)/shard_map/all_to_all | solution.py:249
  50.2 0.0 copy-done
  50.2 1.9 %shard_map.115 = (f32[4,16,128]{2,1,0:T(8,128)}, f32[16,256]{1,0:T(8,128)}) custom-call(f32[1152,128]{1,0:T(8,128)} %bitcast.18), custom_call_target="tpu_custom_call" | custom-call | tf_op jit(solution)/shard_map/pallas_call | solution.py:240
  52.2 8.0 %all-to-all-done.1 = f32[128,1,256]{2,1,0:T(1,128)S(1)} async-done(((f32[128,1,256]{2,1,0:T(1,128)}), f32[128,1,256]{2,1,0:T(1,128)S(1)}, u32[]{:S(2)}, u32[]{:S(2)}) %all-to-all-start.1) | async-done | bytes 131104 | tf_op jit(solution)/shard_map/all_to_all | solution.py:249
  60.2 0.0 copy-start.2
  60.2 0.6 %copy-done.2 = f32[128,1,256]{2,1,0:T(1,128)} copy-done((f32[128,1,256]{2,1,0:T(1,128)}, f32[128,1,256]{2,1,0:T(1,128)S(1)}, u32[]{:S(2)}) %copy-start.2) | copy-done | bytes 131096
  60.8 1.7 %shard_map.116 = f32[5,16,128]{2,1,0:T(8,128)} custom-call(f32[256,128]{1,0:T(8,128)} %bitcast.22, f32[4,16,128]{2,1,0:T(8,128)} %get-tuple-element.17.sums_ref, f32[16,256]{1,0:T(8,128)} %get-tuple-element.18.chosen_ref), custom_call_target="tpu_custom_call" | custom-call | tf_op jit(solution)/shard_map/pallas_call | solution.py:240
Async XLA Ops:
  2.1 15.7 %all-to-all-start = ((f32[8,1,5120]{2,1,0:T(1,128)}), f32[8,1,5120]{2,1,0:T(1,128)S(1)}, u32[]{:S(2)}, u32[]{:S(2)}) async-start(f32[8,1,5120]{2,1,0:T(1,128)} %bitcast.20), calls=%async_computation | async-start | bytes 327680 | tf_op jit(solution)/shard_map/all_to_all | solution.py:249
  17.8 0.7 %copy-start.1 = (f32[8,1,5120]{2,1,0:T(1,128)}, f32[8,1,5120]{2,1,0:T(1,128)S(1)}, u32[]{:S(2)}) copy-start(f32[8,1,5120]{2,1,0:T(1,128)S(1)} %all-to-all-done) | copy-start | bytes 491524
  18.5 22.0 %all-to-all-start.2 = ((f32[128,1,1152]{2,1,0:T(1,128)}), f32[128,1,1152]{2,1,0:T(1,128)S(1)}, u32[]{:S(2)}, u32[]{:S(2)}) async-start(f32[128,1,1152]{2,1,0:T(1,128)} %bitcast.21), calls=%async_computation.2 | async-start | bytes 1179648 | tf_op jit(solution)/shard_map/all_to_all | solution.py:249
  40.5 9.8 %copy-start = (f32[128,1,1152]{2,1,0:T(1,128)}, f32[128,1,1152]{2,1,0:T(1,128)S(1)}, u32[]{:S(2)}) copy-start(f32[128,1,1152]{2,1,0:T(1,128)S(1)} %all-to-all-done.2) | copy-start | bytes 1769476
  40.5 19.7 %all-to-all-start.1 = ((f32[128,1,256]{2,1,0:T(1,128)}), f32[128,1,256]{2,1,0:T(1,128)S(1)}, u32[]{:S(2)}, u32[]{:S(2)}) async-start(f32[128,1,256]{2,1,0:T(1,128)} %bitcast.25), calls=%async_computation.1 | async-start | bytes 262144 | tf_op jit(solution)/shard_map/all_to_all | solution.py:249
  60.2 0.6 %copy-start.2 = (f32[128,1,256]{2,1,0:T(1,128)}, f32[128,1,256]{2,1,0:T(1,128)S(1)}, u32[]{:S(2)}) copy-start(f32[128,1,256]{2,1,0:T(1,128)S(1)} %all-to-all-done.1) | copy-start | bytes 393220

commit v2 on v1

v2 whole, which is shorter than its diff:
```python
import functools

import jax
import jax.numpy as jnp
from jax import lax
from jax.experimental import pallas as pl
from jax.experimental.pallas import tpu as pltpu
from jax.sharding import PartitionSpec as P

BLOCK = 128
VARS = 5
CAP = 2
OB = 16
PEERS = 8
DEVS = 128
LINES = 16
NJ = 256
PQ = 4
PAY = 24
PAN = 12
NU0 = 12
VO0 = 16
ND0 = 18
FR = 11
UNROLL = 8
OWN_UNROLL = 8
F32 = jnp.float32
BF16 = jnp.bfloat16


def iota(shape, axis):
    return lax.broadcasted_iota(jnp.int32, shape, axis)


def split3(v):
    high = v.astype(BF16)
    rest = v - high.astype(F32)
    mid = rest.astype(BF16)
    low = (rest - mid.astype(F32)).astype(BF16)
    return high, mid, low


def onehot(cond):
    return jnp.where(cond, 1.0, 0.0).astype(BF16)


def contract_lanes(a, b):
    return lax.dot_general(a, b, (((1,), (1,)), ((), ())), preferred_element_type=F32)


def halves(rows):
    return jnp.concatenate([rows[:, :BLOCK], rows[:, BLOCK:]], axis=0)


def pack_kernel(nodes_ref, panels_ref, nu_ref, vort_ref, out_ref):
    def fill(base, nu_line, line):
        def put(row, value):
            out_ref[pl.ds(base + row, 1), :] = value

        for c in range(3):
            vec = panels_ref[c]
            for q in range(PQ):
                put(c * PQ + q, vec[:, q * BLOCK : (q + 1) * BLOCK])
        for half in range(2):
            lanes = slice(half * BLOCK, (half + 1) * BLOCK)
            for at in range(2):
                put(NU0 + at * 2 + half, nu_ref[nu_line + at : nu_line + at + 1, lanes])
            put(VO0 + half, vort_ref[line : line + 1, lanes])
            for c in range(3):
                put(ND0 + c * 2 + half, nodes_ref[c, line : line + 1, lanes])

    fill(0, 0, 0)
    first = out_ref[0:PAY, :]
    for s in range(1, PEERS):
        out_ref[s * PAY : (s + 1) * PAY, :] = first
    after = lax.rem(lax.axis_index("blk") + 1, PEERS)
    fill(after * PAY, LINES - 2, LINES - 1)


def panel_terms(raw):
    square = raw[0:4] * raw[0:4] + raw[4:8] * raw[4:8] + raw[8:12] * raw[8:12]
    high, mid, low = [
        t.astype(F32) for t in split3(jnp.concatenate([raw, square], axis=0))
    ]
    none = jnp.zeros_like(high)
    terms = jnp.concatenate([high, high, high, mid, mid, low, none, none], axis=0)
    return terms.T.astype(BF16)


def line_least(coords, lhs):
    c4 = iota((PQ * 4, NJ), 0) // 4
    q4 = iota((PQ * 4, NJ), 0) % 4
    x, y, z = [jnp.broadcast_to(v, (PQ * 4, NJ)) for v in coords]
    base = jnp.where(c4 == 0, x, jnp.where(c4 == 1, y, z)) * -2.0
    base = jnp.where(c4 == 3, 1.0, base)
    best = None
    for q in range(PQ):
        high, mid, low = split3(jnp.where(q4 == q, base, 0.0))
        none = jnp.zeros_like(high)
        w = jnp.concatenate([high, mid, low, high, mid, high, none, none], axis=0)
        rest = jnp.dot(lhs, w, preferred_element_type=F32)
        least = jnp.min(rest.reshape(lhs.shape[0] // 8, 8, NJ), axis=0)
        best = least if best is None else jnp.minimum(best, least)
    return best


def own_kernel(panels_ref, nodes_ref, least_ref, raw_ref, lhs_ref):
    for c in range(3):
        vec = panels_ref[c]
        for q in range(PQ):
            raw_ref[c * PQ + q : c * PQ + q + 1, :] = vec[:, q * BLOCK : (q + 1) * BLOCK]
    lhs_ref[...] = panel_terms(raw_ref[0:PAN, :])

    def line(i, unused):
        best = line_least([nodes_ref[c, pl.ds(i, 1), :] for c in range(3)], lhs_ref[...])
        least_ref[pl.ds(i, 1), :] = jnp.min(best, axis=0, keepdims=True)
        return unused

    lax.fori_loop(0, LINES, line, 0, unroll=OWN_UNROLL)


def route_kernel(owner_ref, block_ref, size_ref, cell_ref, flow_ref, send_ref, pick_ref, live_ref):
    square = (DEVS, DEVS)
    row = iota(square, 0)
    lane = iota(square, 1)
    owner = owner_ref[...]
    hits = onehot(jnp.broadcast_to(owner, square) == row)
    before = onehot(row < lane)
    earlier = jnp.dot(hits, before, preferred_element_type=F32)
    rank = jnp.sum(hits.astype(F32) * earlier, axis=0, keepdims=True)
    slot = owner * CAP + rank.astype(jnp.int32)
    block = block_ref[...]
    place = (block % 2) * LINES + block // 2
    places = onehot((jnp.broadcast_to(place, square) == row % 32) & (row < 96))
    sizes = jnp.broadcast_to(size_ref[...], square).astype(F32).astype(BF16)
    cell = jnp.broadcast_to(cell_ref[...], square)
    state = jnp.concatenate([halves(flow_ref[v]) for v in range(VARS - 1)], axis=1)
    high, mid, low = split3(state)
    table = jnp.concatenate([high, mid, low, jnp.zeros_like(high)], axis=0)
    cells = None
    for r in range(CAP):
        sel = onehot(jnp.broadcast_to(slot, square) == row * CAP + r)
        pick = contract_lanes(sel, places)
        live = jnp.where(lane.astype(F32) < contract_lanes(sel, sizes), 1.0, 0.0)
        named = contract_lanes(sel, onehot((cell == row - r * OB) & (row < (r + 1) * OB)))
        cells = named if cells is None else cells + named
        pick_ref[pl.ds(r * DEVS, DEVS), :] = pick
        live_ref[pl.ds(r * DEVS, DEVS), :] = live
        values = jnp.dot(pick.astype(BF16), table, preferred_element_type=F32)
        for v in range(VARS - 1):
            send_ref[pl.ds(r * VARS + 1 + v, DEVS, stride=FR), :] = (
                values[:, v * BLOCK : (v + 1) * BLOCK] * live
            )
    send_ref[pl.ds(FR - 1, DEVS, stride=FR), :] = cells


def sa_step(centre, east, west, dist, vort):
    lane = iota(centre.shape, 1)
    north = jnp.where(lane == NJ - 1, 0.0, pltpu.roll(centre, NJ - 1, 1))
    south = jnp.where(lane == 0, 0.0, pltpu.roll(centre, 1, 1))
    flux = (1.0 + 0.5 * (centre + east)) * (east - centre) - (1.0 + 0.5 * (centre + west)) * (
        centre - west
    )
    flux = (
        flux
        + (1.0 + 0.5 * (centre + north)) * (north - centre)
        - (1.0 + 0.5 * (centre + south)) * (centre - south)
    )
    grads = 0.25 * ((east - west) * (east - west) + (north - south) * (north - south))
    diffusion = (flux + 0.622 * grads) * 1.5
    ratio = centre / dist
    return centre + 0.02 * (0.1355 * vort * centre - 3.24 * ratio * ratio + diffusion)


def step_kernel(
    got_ref, own_ref, nodes_ref, nu_ref, vort_ref, pick_ref, live_ref, rows_ref,
    dist_ref, next_ref, send_ref,
    lhs_ref, node_ext, nu_ext, vort_ext, dist_ext,
):
    me = lax.axis_index("blk")

    def member(k):
        return pl.multiple_of(lax.rem(me + k, PEERS) * PAY, 8)

    left, right = member(PEERS - 1), member(1)

    def edge(base, row):
        return jnp.concatenate(
            [got_ref[pl.ds(base + row, 1), :], got_ref[pl.ds(base + row + 1, 1), :]], axis=1
        )

    for c in range(3):
        node_ext[c, 1 : 1 + LINES, :] = nodes_ref[c]
        node_ext[c, 0:1, :] = edge(left, ND0 + c * 2)
        node_ext[c, 1 + LINES : 2 + LINES, :] = edge(right, ND0 + c * 2)
    nu_ext[2 : 2 + LINES, :] = nu_ref[...]
    vort_ext[1 : 1 + LINES, :] = vort_ref[...]
    for at in range(2):
        nu_ext[at : at + 1, :] = edge(left, NU0 + at * 2)
        nu_ext[2 + LINES + at : 3 + LINES + at, :] = edge(right, NU0 + at * 2)
    vort_ext[0:1, :] = edge(left, VO0)
    vort_ext[1 + LINES : 2 + LINES, :] = edge(right, VO0)

    for k in range(PEERS):
        raw = got_ref[pl.ds(member(k + 1), PAN), :]
        lhs_ref[k * BLOCK : (k + 1) * BLOCK, :] = panel_terms(raw)

    def finish(i, least):
        x, y, z = [node_ext[c, pl.ds(i, 1), :] for c in range(3)]
        least = jnp.maximum(least + (x * x + y * y + z * z), 0.0)
        dist_ext[pl.ds(i, 1), :] = jnp.sqrt(least + 0.25)

    def coords(i):
        return [node_ext[c, pl.ds(i, 1), :] for c in range(3)]

    def line(i, unused):
        best = line_least(coords(i), lhs_ref[0 : (PEERS - 1) * BLOCK, :])
        best = jnp.minimum(jnp.min(best, axis=0, keepdims=True), own_ref[pl.ds(i - 1, 1), :])
        finish(i, best)
        return unused

    for i in (0, 1 + LINES):
        finish(i, jnp.min(line_least(coords(i), lhs_ref[...]), axis=0, keepdims=True))
    lax.fori_loop(1, 1 + LINES, line, 0, unroll=UNROLL)

    mid_nu = sa_step(
        nu_ext[1 : 3 + LINES, :],
        nu_ext[2 : 4 + LINES, :],
        nu_ext[0 : 2 + LINES, :],
        dist_ext[0 : 2 + LINES, :],
        vort_ext[0 : 2 + LINES, :],
    )
    nu_ext[0 : 2 + LINES, :] = mid_nu
    dist = dist_ext[1 : 1 + LINES, :]
    new = sa_step(
        nu_ext[1 : 1 + LINES, :],
        nu_ext[2 : 2 + LINES, :],
        nu_ext[0:LINES, :],
        dist,
        vort_ref[...],
    )
    dist_ref[...] = dist
    next_ref[...] = new
    high, mid, low = split3(halves(new))
    table = jnp.concatenate([high, mid, low, jnp.zeros_like(high)], axis=0)
    values = jnp.dot(pick_ref[...].astype(BF16), table, preferred_element_type=F32)
    values = values * live_ref[...]
    for r in range(CAP):
        send_ref[pl.ds(r * VARS, DEVS, stride=FR), :] = values[r * DEVS : (r + 1) * DEVS]


def add_up(chosen, rows):
    total = None
    for part in split3(rows):
        term = jnp.dot(chosen, part, preferred_element_type=F32)
        total = term if total is None else total + term
    return total


def sum_kernel(got_ref, out_ref):
    cells = got_ref[pl.ds(FR - 1, DEVS, stride=FR), :].T
    chosen = jnp.concatenate([cells[r * OB : (r + 1) * OB] for r in range(CAP)], axis=1)
    chosen = chosen.astype(BF16)
    for v in range(VARS):
        rows = jnp.concatenate(
            [got_ref[pl.ds(r * VARS + v, DEVS, stride=FR), :] for r in range(CAP)], axis=0
        )
        out_ref[v] = add_up(chosen, rows)


def call(kernel, outs, *args, scratch=(), alias=(), hbm=(), fetch=True):
    if fetch:
        args = [pltpu.with_memory_space_constraint(a, pltpu.VMEM) for a in args]
    vmem = pl.BlockSpec(memory_space=pltpu.VMEM)
    return pl.pallas_call(
        kernel,
        out_shape=tuple(
            (jax.ShapeDtypeStruct if n in hbm else pltpu.VMEM)(shape, F32)
            for n, shape in enumerate(outs)
        ),
        in_specs=[vmem] * len(args),
        out_specs=tuple(vmem for shape in outs),
        scratch_shapes=list(scratch),
        input_output_aliases=dict(alias),
    )(*args)


def exchange(rows, count, axes):
    sent = rows.reshape(count, 1, -1)
    got = lax.all_to_all(sent, axes, split_axis=0, concat_axis=0, tiled=True)
    return got.reshape(rows.shape)


def per_device(
    nodes, panels, nu_field, vorticity, flow, fringe_block, fringe_size, fringe_owner, fringe_cell
):
    nodes, nu, vort, flow = nodes[0], nu_field[0], vorticity[0], flow[0]
    flat = panels.reshape(3, 1, PQ * BLOCK)
    (pay,) = call(
        pack_kernel, [(PEERS * PAY, BLOCK)], nodes, flat, nu, vort, fetch=False
    )
    pay = exchange(pay, PEERS, "blk")
    (own,) = call(
        own_kernel,
        [(LINES, NJ)],
        flat,
        nodes,
        scratch=(pltpu.VMEM((16, BLOCK), F32), pltpu.VMEM((BLOCK, BLOCK), BF16)),
    )
    wide = (1, DEVS)
    send, pick, live = call(
        route_kernel,
        [(DEVS * FR, BLOCK), (DEVS * CAP, BLOCK), (DEVS * CAP, BLOCK)],
        fringe_owner.reshape(wide),
        fringe_block.reshape(wide),
        fringe_size.reshape(wide),
        fringe_cell.reshape(wide),
        flow,
    )
    line = (LINES, NJ)
    ext = pltpu.VMEM((24, NJ), F32)
    dist, nu_next, send = call(
        step_kernel,
        [line, line, (DEVS * FR, BLOCK)],
        pay, own, nodes, nu, vort, pick, live, send,
        scratch=(
            pltpu.VMEM((PEERS * BLOCK, BLOCK), BF16),
            pltpu.VMEM((3, 24, NJ), F32),
            ext, ext, ext,
        ),
        alias=((7, 2),),
        hbm=(0, 1),
    )
    got = exchange(send, DEVS, ("grp", "blk"))
    (offbody,) = call(sum_kernel, [(VARS, OB, BLOCK)], got, hbm=(0,))
    return (dist[None], nu_next[None], jnp.transpose(offbody, (1, 0, 2)))


def solution(mesh):
    in_specs = (
        P("grp", None, "blk", None),
        P("grp", None, "blk"),
        P("grp", "blk", None),
        P("grp", "blk", None),
        P("grp", None, "blk", None),
        P(("grp", "blk")),
        P(("grp", "blk")),
        P(("grp", "blk"), None),
        P(("grp", "blk")),
    )
    out_specs = (P("grp", "blk", None), P("grp", "blk", None), P(("grp", "blk"), None, None))
    return jax.shard_map(
        per_device, mesh=mesh, in_specs=in_specs, out_specs=out_specs, check_vma=False
    )
```

time: 63 us -> 51.9 us (0.82)
  blocking collectives: 0 us -> 22.6 us
  starting transfers between devices: 25 us -> 8.61 us
  waiting for transfers between devices: 12.9 us -> 3.97 us
  Pallas kernels: 22.7 us -> 14.8 us
  local copies, waits for them, and re-layouts: 1.31 us -> 0.68 us
    all_to_all x0 -> x1, blocking collectives: none -> 22.6 us  [exchange(): got = lax.all_to_all(sent, axes, split_axis=0, concat_axis=0, tiled=True)]
    all_to_all x3 -> x1, starting transfers between devices: 25 us -> 8.61 us  [exchange(): got = lax.all_to_all(sent, axes, split_axis=0, concat_axis=0, tiled=True)]
    all_to_all x3 -> x1, waiting for transfers between devices: 12.9 us -> 3.97 us  [exchange(): got = lax.all_to_all(sent, axes, split_axis=0, concat_axis=0, tiled=True)]
    pallas_call x5, Pallas kernels: 22.7 us -> 14.8 us  [call(): pl.pallas_call(kernel, out_shape=tuple(((jax.ShapeDtypeStruct if n in hbm...]
    unnamed x6 -> x18, local copies, waits for them, and re-layouts: 1.31 us -> 0.68 us
  transfers between devices with their start and end apart: 3 -> 1, of which waited for: 2 -> 1; matrix products, arithmetic and copies ran while one was open for 0% -> 0% of each run, Pallas kernels for 31% -> 4%
where the time goes in v2:
time: 51.9 us; the launch traced here: 51.4 us
  blocking collectives  22.6 us (44%)
  Pallas kernels  14.8 us (29%)
  starting transfers between devices  8.61 us (17%)
  waiting for transfers between devices  3.97 us (8%)
  between operations  0.71 us (1%)
  local copies, waits for them, and re-layouts  0.68 us (1%)
    all_to_all x1, blocking collectives, exchange(): got = lax.all_to_all(sent, axes, split_axis=0, concat_axis=0, tiled=True)  22.6 us
    pallas_call x5, Pallas kernels, call(): pl.pallas_call(kernel, out_shape=tuple(((jax.ShapeDtypeStruct if n in hbm...  14.8 us
    all_to_all x1, starting transfers between devices, exchange(): got = lax.all_to_all(sent, axes, split_axis=0, concat_axis=0, tiled=True)  8.61 us
    all_to_all x1, waiting for transfers between devices, exchange(): got = lax.all_to_all(sent, axes, split_axis=0, concat_axis=0, tiled=True)  3.97 us
  transfers between devices with their start and end apart: 1, of which 1 were waited for; matrix products, arithmetic and copies ran while one was open for 0% of the time, Pallas kernels for 4%

profile of v2, /device:TPU:1, one launch (start us, length us, event | category | flops | bytes accessed | tf_op | source)
XLA Modules:
  0.0 51.4 jit_solution(7151392406854569344)
XLA Ops:
  0.6 1.5 %shard_map.112 = f32[192,128]{1,0:T(8,128)} custom-call(f32[3,16,256]{2,1,0:T(8,128)} %bitcast.18, f32[3,1,512]{2,1,0:T(1,128)} %bitcast.27, f32[16,256]{1,0:T(8,128)} %bitcast.22, f32[16,256]{1,0:T(8,128)} %bitcast.24), custom_call_target="tpu_custom_call" | custom-call | tf_op jit(solution)/shard_map/pallas_call | solution.py:275
  2.1 0.0 copy-start.4
  2.1 8.6 %all-to-all-start = ((f32[8,1,3072]{2,1,0:T(1,128)}), f32[8,1,3072]{2,1,0:T(1,128)S(1)}, u32[]{:S(2)}, u32[]{:S(2)}) async-start(f32[8,1,3072]{2,1,0:T(1,128)} %bitcast.4), calls=%async_computation | async-start | bytes 196608 | tf_op jit(solution)/shard_map/all_to_all | solution.py:290
  10.7 0.0 copy-done
  10.7 0.0 copy-done.4
  10.7 0.0 copy-start.3
  10.8 1.6 %shard_map.113.own_ref = f32[16,256]{1,0:T(8,128)S(1)} custom-call(f32[3,1,512]{2,1,0:T(1,128)S(1)} %bitcast.28, f32[3,16,256]{2,1,0:T(8,128)S(1)} %bitcast.19), custom_call_target="tpu_custom_call" | custom-call | tf_op jit(solution)/shard_map/pallas_call | solution.py:275
  12.3 0.0 copy-start.8
  12.3 0.0 copy-start.5
  12.3 0.0 copy-start.6
  12.4 0.0 copy-start.7
  12.4 0.0 copy-done.3
  12.4 0.6 %copy-done.8 = s32[128]{0:T(128)S(1)} copy-done((s32[128]{0:T(128)S(1)}, s32[128]{0:T(128)}, u32[]{:S(2)}) %copy-start.8) | copy-done | bytes 536
  13.0 0.0 copy-done.5
  13.0 0.0 copy-done.6
  13.0 0.0 copy-done.7
  13.0 0.0 copy-start.1
  13.0 0.6 %shard_map.114 = (f32[1408,128]{1,0:T(8,128)S(1)}, f32[256,128]{1,0:T(8,128)S(1)}, f32[256,128]{1,0:T(8,128)S(1)}) custom-call(s32[1,128]{1,0:T(1,128)S(1)} %bitcast.29, s32[1,128]{1,0:T(1,128)S(1)} %bitcast.30, s32[1,128]{1,0:T(1,128)S(1)} %bitcast.31, s32[1,128]{1,0:T(1,128)S(1)} %bitcast.32, f32[4,16,256]{2,1,0:T(8,128)S(1)} %bitcast.26), custom_call_target="tpu_custom_call" | custom-call | tf_op jit(solution)/shard_map/pallas_call | solution.py:275
  13.6 4.0 %all-to-all-done = f32[8,1,3072]{2,1,0:T(1,128)S(1)} async-done(((f32[8,1,3072]{2,1,0:T(1,128)}), f32[8,1,3072]{2,1,0:T(1,128)S(1)}, u32[]{:S(2)}, u32[]{:S(2)}) %all-to-all-start) | async-done | bytes 98336 | tf_op jit(solution)/shard_map/all_to_all | solution.py:290
  17.6 0.0 copy-done.1
  17.6 0.0 copy-done.2
  17.6 10.2 %shard_map.115 = (f32[16,256]{1,0:T(8,128)}, f32[16,256]{1,0:T(8,128)}, f32[1408,128]{1,0:T(8,128)S(1)}) custom-call(f32[192,128]{1,0:T(8,128)S(1)} %bitcast.21, f32[16,256]{1,0:T(8,128)S(1)} %shard_map.113.own_ref, f32[3,16,256]{2,1,0:T(8,128)S(1)} %bitcast.20, f32[16,256]{1,0:T(8,128)S(1)} %bitcast.23, ...), custom_call_target="tpu_custom_call", output_to_operand_aliasing={{2}: (7, {})} | custom-call | tf_op jit(solution)/shard_map/pallas_call | solution.py:275
  27.8 22.6 %all_to_all.10 = f32[128,1,1408]{2,1,0:T(1,128)S(1)} all-to-all(f32[128,1,1408]{2,1,0:T(1,128)S(1)} %bitcast.16), channel_id=1, replica_groups=mesh['grp'=16,'blk'=8] {'grp','blk'}, dimensions={0} | all-to-all | bytes 1441792 | tf_op jit(solution)/shard_map/all_to_all | solution.py:290
  50.4 0.9 %shard_map.116 = f32[5,16,128]{2,1,0:T(8,128)} custom-call(f32[1408,128]{1,0:T(8,128)S(1)} %bitcast.17), custom_call_target="tpu_custom_call" | custom-call | tf_op jit(solution)/shard_map/pallas_call | solution.py:275
  (2 shorter events, 0.0 us)
Async XLA Ops:
  2.1 8.6 %copy-start = (f32[1,3,16,256]{3,2,1,0:T(8,128)S(1)}, f32[1,3,16,256]{3,2,1,0:T(8,128)}, u32[]{:S(2)}) copy-start(f32[1,3,16,256]{3,2,1,0:T(8,128)} %param.9) | copy-start | bytes 147460
  2.1 8.6 %copy-start.4 = (f32[1,3,512]{2,0,1:T(1,128)S(1)}, f32[1,3,512]{2,0,1:T(1,128)}, u32[]{:S(2)}) copy-start(f32[1,3,512]{2,0,1:T(1,128)} %param.10) | copy-start | bytes 18436
  2.1 15.5 %all-to-all-start = ((f32[8,1,3072]{2,1,0:T(1,128)}), f32[8,1,3072]{2,1,0:T(1,128)S(1)}, u32[]{:S(2)}, u32[]{:S(2)}) async-start(f32[8,1,3072]{2,1,0:T(1,128)} %bitcast.4), calls=%async_computation | async-start | bytes 196608 | tf_op jit(solution)/shard_map/all_to_all | solution.py:290
  10.7 1.6 %copy-start.3 = (f32[1,4,16,256]{3,2,1,0:T(8,128)S(1)}, f32[1,4,16,256]{3,2,1,0:T(8,128)}, u32[]{:S(2)}) copy-start(f32[1,4,16,256]{3,2,1,0:T(8,128)} %param.13) | copy-start | bytes 196612
  12.3 0.7 %copy-start.8 = (s32[128]{0:T(128)S(1)}, s32[128]{0:T(128)}, u32[]{:S(2)}) copy-start(s32[128]{0:T(128)} %param.17) | copy-start | bytes 1540
  12.3 0.7 %copy-start.5 = (s32[128,1]{0,1:T(1,128)S(1)}, s32[128,1]{0,1:T(1,128)}, u32[]{:S(2)}) copy-start(s32[128,1]{0,1:T(1,128)} %param.16) | copy-start | bytes 1540
  12.3 0.7 %copy-start.6 = (s32[128]{0:T(128)S(1)}, s32[128]{0:T(128)}, u32[]{:S(2)}) copy-start(s32[128]{0:T(128)} %param.14) | copy-start | bytes 1540
  12.4 0.7 %copy-start.7 = (s32[128]{0:T(128)S(1)}, s32[128]{0:T(128)}, u32[]{:S(2)}) copy-start(s32[128]{0:T(128)} %param.15) | copy-start | bytes 1540
  13.0 4.6 %copy-start.1 = (f32[1,16,256]{2,1,0:T(8,128)S(1)}, f32[1,16,256]{2,1,0:T(8,128)}, u32[]{:S(2)}) copy-start(f32[1,16,256]{2,1,0:T(8,128)} %param.11) | copy-start | bytes 49156
  13.0 4.6 %copy-start.2 = (f32[1,16,256]{2,1,0:T(8,128)S(1)}, f32[1,16,256]{2,1,0:T(8,128)}, u32[]{:S(2)}) copy-start(f32[1,16,256]{2,1,0:T(8,128)} %param.12) | copy-start | bytes 49156

commit v3 on v2

--- a/solution.py
+++ b/solution.py
@@ -16,14 +16,14 @@
 LINES = 16
 NJ = 256
 PQ = 4
-PAY = 24
 PAN = 12
-NU0 = 12
-VO0 = 16
-ND0 = 18
+EDGE = 12
+PAY = 40
+NEAR = 36
 FR = 11
-UNROLL = 8
-OWN_UNROLL = 8
+UNROLL = 16
+OWN_UNROLL = 16
+FLIP = 69
 F32 = jnp.float32
 BF16 = jnp.bfloat16
 
@@ -53,28 +53,32 @@
 
 
 def pack_kernel(nodes_ref, panels_ref, nu_ref, vort_ref, out_ref):
-    def fill(base, nu_line, line):
-        def put(row, value):
-            out_ref[pl.ds(base + row, 1), :] = value
-
-        for c in range(3):
-            vec = panels_ref[c]
-            for q in range(PQ):
-                put(c * PQ + q, vec[:, q * BLOCK : (q + 1) * BLOCK])
+    def put(row, value):
+        out_ref[pl.ds(row, 1), :] = value
+
+    for c in range(3):
+        vec = panels_ref[c]
+        for q in range(PQ):
+            put(c * PQ + q, vec[:, q * BLOCK : (q + 1) * BLOCK])
+    odd = lax.rem(lax.axis_index("blk"), 2)
+    for base, nu_line, line in (
+        (PAN + EDGE * (1 - odd), 0, 0),
+        (PAN + EDGE * odd, LINES - 2, LINES - 1),
+    ):
         for half in range(2):
             lanes = slice(half * BLOCK, (half + 1) * BLOCK)
             for at in range(2):
-                put(NU0 + at * 2 + half, nu_ref[nu_line + at : nu_line + at + 1, lanes])
-            put(VO0 + half, vort_ref[line : line + 1, lanes])
+                put(base + at * 2 + half, nu_ref[nu_line + at : nu_line + at + 1, lanes])
+            put(base + 4 + half, vort_ref[line : line + 1, lanes])
             for c in range(3):
-                put(ND0 + c * 2 + half, nodes_ref[c, line : line + 1, lanes])
-
-    fill(0, 0, 0)
-    first = out_ref[0:PAY, :]
-    for s in range(1, PEERS):
-        out_ref[s * PAY : (s + 1) * PAY, :] = first
-    after = lax.rem(lax.axis_index("blk") + 1, PEERS)
-    fill(after * PAY, LINES - 2, LINES - 1)
+                put(base + 6 + c * 2 + half, nodes_ref[c, line : line + 1, lanes])
+    out_ref[PAN + 2 * EDGE :, :] = jnp.zeros((PAY - PAN - 2 * EDGE, BLOCK), F32)
+
+
+def join_kernel(pay_ref, mate_ref, least_ref, near_ref):
+    near_ref[0:PAN, :] = pay_ref[0:PAN, :]
+    near_ref[PAN : 2 * PAN, :] = mate_ref[0:PAN, :]
+    near_ref[2 * PAN : NEAR, :] = mate_ref[PAN + EDGE : PAN + 2 * EDGE, :]
 
 
 def panel_terms(raw):
@@ -104,22 +108,38 @@
     return best
 
 
-def own_kernel(panels_ref, nodes_ref, least_ref, raw_ref, lhs_ref):
+def lines_least(nodes_ref, lhs_ref, least_ref, before):
+    def line(i, unused):
+        best = line_least([nodes_ref[c, pl.ds(i, 1), :] for c in range(3)], lhs_ref[...])
+        best = jnp.min(best, axis=0, keepdims=True)
+        if before is not None:
+            best = jnp.minimum(best, before[pl.ds(i, 1), :])
+        least_ref[pl.ds(i, 1), :] = best
+        return unused
+
+    lax.fori_loop(0, LINES, line, 0, unroll=OWN_UNROLL)
+
+
+def own_least(panels_ref, nodes_ref, least_ref, raw_ref, lhs_ref):
     for c in range(3):
         vec = panels_ref[c]
         for q in range(PQ):
             raw_ref[c * PQ + q : c * PQ + q + 1, :] = vec[:, q * BLOCK : (q + 1) * BLOCK]
     lhs_ref[...] = panel_terms(raw_ref[0:PAN, :])
-
-    def line(i, unused):
-        best = line_least([nodes_ref[c, pl.ds(i, 1), :] for c in range(3)], lhs_ref[...])
-        least_ref[pl.ds(i, 1), :] = jnp.min(best, axis=0, keepdims=True)
-        return unused
-
-    lax.fori_loop(0, LINES, line, 0, unroll=OWN_UNROLL)
-
-
-def route_kernel(owner_ref, block_ref, size_ref, cell_ref, flow_ref, send_ref, pick_ref, live_ref):
+    lines_least(nodes_ref, lhs_ref, least_ref, None)
+
+
+def mate_kernel(mate_ref, nodes_ref, own_ref, least_ref, lhs_ref):
+    lhs_ref[...] = panel_terms(mate_ref[0:PAN, :])
+    lines_least(nodes_ref, lhs_ref, least_ref, own_ref)
+
+
+def early_kernel(
+    panels_ref, nodes_ref, owner_ref, block_ref, size_ref, cell_ref, flow_ref,
+    least_ref, send_ref, pick_ref, live_ref,
+    raw_ref, lhs_ref,
+):
+    own_least(panels_ref, nodes_ref, least_ref, raw_ref, lhs_ref)
     square = (DEVS, DEVS)
     row = iota(square, 0)
     lane = iota(square, 1)
@@ -128,7 +148,7 @@
     before = onehot(row < lane)
     earlier = jnp.dot(hits, before, preferred_element_type=F32)
     rank = jnp.sum(hits.astype(F32) * earlier, axis=0, keepdims=True)
-    slot = owner * CAP + rank.astype(jnp.int32)
+    slot = (owner ^ FLIP) * CAP + rank.astype(jnp.int32)
     block = block_ref[...]
     place = (block % 2) * LINES + block // 2
     places = onehot((jnp.broadcast_to(place, square) == row % 32) & (row < 96))
@@ -173,37 +193,40 @@
 
 
 def step_kernel(
-    got_ref, own_ref, nodes_ref, nu_ref, vort_ref, pick_ref, live_ref, rows_ref,
+    pay_ref, mate_ref, three_ref, one_ref, two_ref, done_ref, nodes_ref, nu_ref, vort_ref, pick_ref, live_ref, rows_ref,
     dist_ref, next_ref, send_ref,
     lhs_ref, node_ext, nu_ext, vort_ext, dist_ext,
 ):
     me = lax.axis_index("blk")
-
-    def member(k):
-        return pl.multiple_of(lax.rem(me + k, PEERS) * PAY, 8)
-
-    left, right = member(PEERS - 1), member(1)
-
-    def edge(base, row):
-        return jnp.concatenate(
-            [got_ref[pl.ds(base + row, 1), :], got_ref[pl.ds(base + row + 1, 1), :]], axis=1
+    even = lax.rem(me, 2) == 0
+    outer_in_one = lax.rem(me + me // 2, 2) == 1
+
+    def edge(left, row):
+        def lines(ref, at):
+            return jnp.concatenate([ref[at : at + 1, :], ref[at + 1 : at + 2, :]], axis=1)
+
+        outer = jnp.where(
+            outer_in_one, lines(one_ref, 2 * PAN + row), lines(three_ref, 2 * PAN + row)
         )
+        inner = lines(mate_ref, PAN + row)
+        return jnp.where(even, outer, inner) if left else jnp.where(even, inner, outer)
 
     for c in range(3):
         node_ext[c, 1 : 1 + LINES, :] = nodes_ref[c]
-        node_ext[c, 0:1, :] = edge(left, ND0 + c * 2)
-        node_ext[c, 1 + LINES : 2 + LINES, :] = edge(right, ND0 + c * 2)
+        node_ext[c, 0:1, :] = edge(True, 6 + c * 2)
+        node_ext[c, 1 + LINES : 2 + LINES, :] = edge(False, 6 + c * 2)
     nu_ext[2 : 2 + LINES, :] = nu_ref[...]
     vort_ext[1 : 1 + LINES, :] = vort_ref[...]
     for at in range(2):
-        nu_ext[at : at + 1, :] = edge(left, NU0 + at * 2)
-        nu_ext[2 + LINES + at : 3 + LINES + at, :] = edge(right, NU0 + at * 2)
-    vort_ext[0:1, :] = edge(left, VO0)
-    vort_ext[1 + LINES : 2 + LINES, :] = edge(right, VO0)
-
-    for k in range(PEERS):
-        raw = got_ref[pl.ds(member(k + 1), PAN), :]
-        lhs_ref[k * BLOCK : (k + 1) * BLOCK, :] = panel_terms(raw)
+        nu_ext[at : at + 1, :] = edge(True, at * 2)
+        nu_ext[2 + LINES + at : 3 + LINES + at, :] = edge(False, at * 2)
+    vort_ext[0:1, :] = edge(True, 4)
+    vort_ext[1 + LINES : 2 + LINES, :] = edge(False, 4)
+
+    sources = [(ref, at) for ref in (one_ref, two_ref, three_ref) for at in (0, PAN)]
+    sources += [(pay_ref, 0), (mate_ref, 0)]
+    for k, (ref, at) in enumerate(sources):
+        lhs_ref[k * BLOCK : (k + 1) * BLOCK, :] = panel_terms(ref[at : at + PAN, :])
 
     def finish(i, least):
         x, y, z = [node_ext[c, pl.ds(i, 1), :] for c in range(3)]
@@ -214,8 +237,8 @@
         return [node_ext[c, pl.ds(i, 1), :] for c in range(3)]
 
     def line(i, unused):
-        best = line_least(coords(i), lhs_ref[0 : (PEERS - 1) * BLOCK, :])
-        best = jnp.minimum(jnp.min(best, axis=0, keepdims=True), own_ref[pl.ds(i - 1, 1), :])
+        best = line_least(coords(i), lhs_ref[0 : (PEERS - 2) * BLOCK, :])
+        best = jnp.minimum(jnp.min(best, axis=0, keepdims=True), done_ref[pl.ds(i - 1, 1), :])
         finish(i, best)
         return unused
 
@@ -285,9 +308,9 @@
     )(*args)
 
 
-def exchange(rows, count, axes):
+def exchange(rows, count, axes, groups=None):
     sent = rows.reshape(count, 1, -1)
-    got = lax.all_to_all(sent, axes, split_axis=0, concat_axis=0, tiled=True)
+    got = lax.all_to_all(sent, axes, split_axis=0, concat_axis=0, tiled=True, axis_index_groups=groups)
     return got.reshape(rows.shape)
 
 
@@ -296,42 +319,47 @@
 ):
     nodes, nu, vort, flow = nodes[0], nu_field[0], vorticity[0], flow[0]
     flat = panels.reshape(3, 1, PQ * BLOCK)
-    (pay,) = call(
-        pack_kernel, [(PEERS * PAY, BLOCK)], nodes, flat, nu, vort, fetch=False
-    )
-    pay = exchange(pay, PEERS, "blk")
-    (own,) = call(
-        own_kernel,
-        [(LINES, NJ)],
+    (pay,) = call(pack_kernel, [(PAY, BLOCK)], nodes, flat, nu, vort, fetch=False)
+    ring = range(PEERS)
+    mate = lax.ppermute(pay, "blk", [(i, i ^ 1) for i in ring])
+    block = pltpu.VMEM((BLOCK, BLOCK), BF16)
+    line = (LINES, NJ)
+    wide = (1, DEVS)
+    own, send, pick, live = call(
+        early_kernel,
+        [line, (DEVS * FR, BLOCK), (DEVS * CAP, BLOCK), (DEVS * CAP, BLOCK)],
         flat,
         nodes,
-        scratch=(pltpu.VMEM((16, BLOCK), F32), pltpu.VMEM((BLOCK, BLOCK), BF16)),
-    )
-    wide = (1, DEVS)
-    send, pick, live = call(
-        route_kernel,
-        [(DEVS * FR, BLOCK), (DEVS * CAP, BLOCK), (DEVS * CAP, BLOCK)],
         fringe_owner.reshape(wide),
         fringe_block.reshape(wide),
         fringe_size.reshape(wide),
         fringe_cell.reshape(wide),
         flow,
-    )
-    line = (LINES, NJ)
+        scratch=(pltpu.VMEM((16, BLOCK), F32), block),
+    )
+    (near,) = call(join_kernel, [(NEAR, BLOCK)], pay, mate, own)
+
+    def swap(mask):
+        return lax.ppermute(near, "blk", [(i, i ^ mask) for i in ring])
+
+    three = swap(6)
+    two = swap(4)
+    one = swap(2)
+    (done,) = call(mate_kernel, [line], mate, nodes, own, scratch=(block,))
     ext = pltpu.VMEM((24, NJ), F32)
     dist, nu_next, send = call(
         step_kernel,
         [line, line, (DEVS * FR, BLOCK)],
-        pay, own, nodes, nu, vort, pick, live, send,
+        pay, mate, three, one, two, done, nodes, nu, vort, pick, live, send,
         scratch=(
             pltpu.VMEM((PEERS * BLOCK, BLOCK), BF16),
             pltpu.VMEM((3, 24, NJ), F32),
             ext, ext, ext,
         ),
-        alias=((7, 2),),
+        alias=((11, 2),),
         hbm=(0, 1),
     )
-    got = exchange(send, DEVS, ("grp", "blk"))
+    got = exchange(send, DEVS, ("grp", "blk"), [[i ^ FLIP for i in range(DEVS)]])
     (offbody,) = call(sum_kernel, [(VARS, OB, BLOCK)], got, hbm=(0,))
     return (dist[None], nu_next[None], jnp.transpose(offbody, (1, 0, 2)))
 

time: 51.9 us -> 50.1 us (0.965)
  blocking collectives: 22.6 us -> 24.1 us
  waiting for transfers between devices: 3.97 us -> 2.5 us
  Pallas kernels: 14.8 us -> 13.6 us
    all_to_all x1 -> x0, starting transfers between devices: 8.61 us -> none  [exchange(): got = lax.all_to_all(sent, axes, split_axis=0, concat_axis=0, tiled=True)]
    ppermute x0 -> x4, starting transfers between devices: none -> 8.23 us  [the longest x3 4.42 us: swap(): return lax.ppermute(near, 'blk', [(i, i ^ mask) for i in ring])]
    all_to_all x1 -> x0, waiting for transfers between devices: 3.97 us -> none  [exchange(): got = lax.all_to_all(sent, axes, split_axis=0, concat_axis=0, tiled=True)]
    ppermute x0 -> x4, waiting for transfers between devices: none -> 2.5 us  [the longest x3 2.5 us: swap(): return lax.ppermute(near, 'blk', [(i, i ^ mask) for i in ring])]
    all_to_all x1, blocking collectives: 22.6 us -> 24.1 us  [exchange(): lax.all_to_all(sent, axes, split_axis=0, concat_axis=0, tiled=True, axis_...]
    pallas_call x5 -> x6, Pallas kernels: 14.8 us -> 13.6 us  [call(): pl.pallas_call(kernel, out_shape=tuple(((jax.ShapeDtypeStruct if n in hbm...]
  transfers between devices with their start and end apart: 1 -> 4, of which waited for: 1 -> 2; matrix products, arithmetic and copies ran while one was open for 0% -> 0% of each run, Pallas kernels for 4% -> 6%
where the time goes in v3:
time: 50.1 us; the launch traced here: 49.9 us
  blocking collectives  24.1 us (48%)
  Pallas kernels  13.6 us (27%)
  starting transfers between devices  8.23 us (16%)
  waiting for transfers between devices  2.5 us (5%)
  between operations  0.73 us (1%)
  local copies, waits for them, and re-layouts  0.69 us (1%)
    all_to_all x1, blocking collectives, exchange(): lax.all_to_all(sent, axes, split_axis=0, concat_axis=0, tiled=True, axis_...  24.1 us
    pallas_call x6, Pallas kernels, call(): pl.pallas_call(kernel, out_shape=tuple(((jax.ShapeDtypeStruct if n in hbm...  13.6 us
    ppermute x3, starting transfers between devices, swap(): return lax.ppermute(near, 'blk', [(i, i ^ mask) for i in ring])  4.42 us
    ppermute x1, starting transfers between devices, per_device(): mate = lax.ppermute(pay, 'blk', [(i, i ^ 1) for i in ring])  3.81 us
    ppermute x3, waiting for transfers between devices, swap(): return lax.ppermute(near, 'blk', [(i, i ^ mask) for i in ring])  2.5 us
  transfers between devices with their start and end apart: 4, of which 2 were waited for; matrix products, arithmetic and copies ran while one was open for 0% of the time, Pallas kernels for 6%

profile of v3, /device:TPU:1, one launch (start us, length us, event | category | flops | bytes accessed | tf_op | source)
XLA Modules:
  0.0 49.9 jit_solution(7978321840714718871)
XLA Ops:
  0.6 0.0 copy-start.3
  0.6 0.0 copy-start
  0.6 0.9 %shard_map.112.pay_ref = f32[40,128]{1,0:T(8,128)S(1)} custom-call(f32[3,16,256]{2,1,0:T(8,128)} %bitcast.16, f32[3,1,512]{2,1,0:T(1,128)} %bitcast.25, f32[16,256]{1,0:T(8,128)} %bitcast.20, f32[16,256]{1,0:T(8,128)} %bitcast.22), custom_call_target="tpu_custom_call" | custom-call | tf_op jit(solution)/shard_map/pallas_call | solution.py:298
  1.5 0.0 copy-start.4
  1.6 3.8 %collective-permute-start = (f32[40,128]{1,0:T(8,128)S(1)}, f32[40,128]{1,0:T(8,128)S(1)}, u32[]{:S(2)}, u32[]{:S(2)}) collective-permute-start(f32[40,128]{1,0:T(8,128)S(1)} %shard_map.112.pay_ref), channel_id=1, source_target_pairs={{0,1},{1,0},{2,3},{3,2},{4,5},{5,4},{6,7},{7,6},{8,9},{9,8},{10,11... | collective-permute-start | bytes 61448 | tf_op jit(solution)/shard_map/ppermute | solution.py:324
  5.4 0.0 copy-done.3
  5.4 0.0 copy-done
  5.4 0.6 %copy-done.8 = s32[128]{0:T(128)S(1)} copy-done((s32[128]{0:T(128)S(1)}, s32[128]{0:T(128)}, u32[]{:S(2)}) %copy-start.8) | copy-done | bytes 536
  6.0 0.0 copy-done.5
  6.0 0.0 copy-done.6
  6.1 0.0 copy-done.7
  6.1 1.8 %shard_map.113 = (f32[16,256]{1,0:T(8,128)S(1)}, f32[1408,128]{1,0:T(8,128)S(1)}, f32[256,128]{1,0:T(8,128)S(1)}, f32[256,128]{1,0:T(8,128)S(1)}) custom-call(f32[3,1,512]{2,1,0:T(1,128)S(1)} %bitcast.26, f32[3,16,256]{2,1,0:T(8,128)S(1)} %bitcast.17, s32[1,128]{1,0:T(1,128)S(1)} %bitcast.27, s32[1,128]{1,0:T(1,128)S(1)} %bitcast.28, s32[1,128]{1,0:T(1,128)S(1)} %bitcast.29, ...), custom_call_target="tpu_custom_call" | custom-call | tf_op jit(solution)/shard_map/pallas_call | solution.py:298
  7.9 0.0 collective-permute-done.mate_ref
  7.9 3.7 %collective-permute-start.3 = (f32[36,128]{1,0:T(8,128)S(1)}, f32[36,128]{1,0:T(8,128)S(1)}, u32[]{:S(2)}, u32[]{:S(2)}) collective-permute-start(f32[36,128]{1,0:T(8,128)S(1)} %shard_map.114), channel_id=1, source_target_pairs={{0,4},{1,5},{2,6},{3,7},{4,0},{5,1},{6,2},{7,3},{8,12},{9,13},{10,... | collective-permute-start | bytes 55304 | tf_op jit(solution)/shard_map/ppermute | solution.py:343
  11.6 0.7 %collective-permute-start.2 = (f32[36,128]{1,0:T(8,128)S(1)}, f32[36,128]{1,0:T(8,128)S(1)}, u32[]{:S(2)}, u32[]{:S(2)}) collective-permute-start(f32[36,128]{1,0:T(8,128)S(1)} %shard_map.114), channel_id=1, source_target_pairs={{0,2},{1,3},{2,0},{3,1},{4,6},{5,7},{6,4},{7,5},{8,10},{9,11},{10,... | collective-permute-start | bytes 55304 | tf_op jit(solution)/shard_map/ppermute | solution.py:343
  12.3 0.0 collective-permute-start.1
  12.3 1.3 %shard_map.115.done_ref = f32[16,256]{1,0:T(8,128)S(1)} custom-call(f32[40,128]{1,0:T(8,128)S(1)} %collective-permute-done.mate_ref, f32[3,16,256]{2,1,0:T(8,128)S(1)} %bitcast.18, f32[16,256]{1,0:T(8,128)S(1)} %get-tuple-element.10.least_ref.own_ref), custom_call_target="tpu_custom_call" | custom-call | tf_op jit(solution)/shard_map/pallas_call | solution.py:298
  13.6 0.0 collective-permute-done.3.two_ref
  13.7 0.5 %collective-permute-done.2.one_ref = f32[36,128]{1,0:T(8,128)S(1)} collective-permute-done((f32[36,128]{1,0:T(8,128)S(1)}, f32[36,128]{1,0:T(8,128)S(1)}, u32[]{:S(2)}, u32[]{:S(2)}) %collective-permute-start.2) | collective-permute-done | bytes 18464 | tf_op jit(solution)/shard_map/ppermute | solution.py:343
  14.2 1.9 %collective-permute-done.1.three_ref = f32[36,128]{1,0:T(8,128)S(1)} collective-permute-done((f32[36,128]{1,0:T(8,128)S(1)}, f32[36,128]{1,0:T(8,128)S(1)}, u32[]{:S(2)}, u32[]{:S(2)}) %collective-permute-start.1) | collective-permute-done | bytes 18464 | tf_op jit(solution)/shard_map/ppermute | solution.py:343
  16.1 0.0 copy-done.1
  16.2 8.7 %shard_map.116 = (f32[16,256]{1,0:T(8,128)}, f32[16,256]{1,0:T(8,128)}, f32[1408,128]{1,0:T(8,128)S(1)}) custom-call(f32[40,128]{1,0:T(8,128)S(1)} %shard_map.112.pay_ref, f32[40,128]{1,0:T(8,128)S(1)} %collective-permute-done.mate_ref, f32[36,128]{1,0:T(8,128)S(1)} %collective-permute-done.1.three_ref, ...), custom_call_target="tpu_custom_call", output_to_operand_aliasing={{2}: (11, {})} | custom-call | tf_op jit(solution)/shard_map/pallas_call | solution.py:298
  24.9 24.1 %all_to_all.5 = f32[128,1,1408]{2,1,0:T(1,128)S(1)} all-to-all(f32[128,1,1408]{2,1,0:T(1,128)S(1)} %bitcast.14), channel_id=1, replica_groups={{69,68,71,70,65,64,67,66,77,76,79,78,73,72,75,74,85,84,87,86,81,80,83,8..., dimensions={0} | all-to-all | bytes 1441792 | tf_op jit(solution)/shard_map/all_to_all | solution.py:313
  48.9 0.9 %shard_map.117 = f32[5,16,128]{2,1,0:T(8,128)} custom-call(f32[1408,128]{1,0:T(8,128)S(1)} %bitcast.15), custom_call_target="tpu_custom_call" | custom-call | tf_op jit(solution)/shard_map/pallas_call | solution.py:298
  (9 shorter events, 0.0 us)
Async XLA Ops:
  0.6 4.7 %copy-start.3 = (f32[1,4,16,256]{3,2,1,0:T(8,128)S(1)}, f32[1,4,16,256]{3,2,1,0:T(8,128)}, u32[]{:S(2)}) copy-start(f32[1,4,16,256]{3,2,1,0:T(8,128)} %param.13) | copy-start | bytes 196612
  0.6 4.7 %copy-start = (f32[1,3,16,256]{3,2,1,0:T(8,128)S(1)}, f32[1,3,16,256]{3,2,1,0:T(8,128)}, u32[]{:S(2)}) copy-start(f32[1,3,16,256]{3,2,1,0:T(8,128)} %param.9) | copy-start | bytes 147460
  1.5 3.9 %copy-start.4 = (f32[1,3,512]{2,0,1:T(1,128)S(1)}, f32[1,3,512]{2,0,1:T(1,128)}, u32[]{:S(2)}) copy-start(f32[1,3,512]{2,0,1:T(1,128)} %param.10) | copy-start | bytes 18436
  1.6 6.3 %collective-permute-start = (f32[40,128]{1,0:T(8,128)S(1)}, f32[40,128]{1,0:T(8,128)S(1)}, u32[]{:S(2)}, u32[]{:S(2)}) collective-permute-start(f32[40,128]{1,0:T(8,128)S(1)} %shard_map.112.pay_ref), channel_id=1, source_target_pairs={{0,1},{1,0},{2,3},{3,2},{4,5},{5,4},{6,7},{7,6},{8,9},{9,8},{10,11... | collective-permute-start | bytes 61448 | tf_op jit(solution)/shard_map/ppermute | solution.py:324
  5.4 0.7 %copy-start.8 = (s32[128]{0:T(128)S(1)}, s32[128]{0:T(128)}, u32[]{:S(2)}) copy-start(s32[128]{0:T(128)} %param.17) | copy-start | bytes 1540
  5.4 0.7 %copy-start.5 = (s32[128,1]{0,1:T(1,128)S(1)}, s32[128,1]{0,1:T(1,128)}, u32[]{:S(2)}) copy-start(s32[128,1]{0,1:T(1,128)} %param.16) | copy-start | bytes 1540
  5.4 0.7 %copy-start.6 = (s32[128]{0:T(128)S(1)}, s32[128]{0:T(128)}, u32[]{:S(2)}) copy-start(s32[128]{0:T(128)} %param.14) | copy-start | bytes 1540
  5.4 0.7 %copy-start.7 = (s32[128]{0:T(128)S(1)}, s32[128]{0:T(128)}, u32[]{:S(2)}) copy-start(s32[128]{0:T(128)} %param.15) | copy-start | bytes 1540
  7.9 5.8 %collective-permute-start.3 = (f32[36,128]{1,0:T(8,128)S(1)}, f32[36,128]{1,0:T(8,128)S(1)}, u32[]{:S(2)}, u32[]{:S(2)}) collective-permute-start(f32[36,128]{1,0:T(8,128)S(1)} %shard_map.114), channel_id=1, source_target_pairs={{0,4},{1,5},{2,6},{3,7},{4,0},{5,1},{6,2},{7,3},{8,12},{9,13},{10,... | collective-permute-start | bytes 55304 | tf_op jit(solution)/shard_map/ppermute | solution.py:343
  11.6 2.6 %collective-permute-start.2 = (f32[36,128]{1,0:T(8,128)S(1)}, f32[36,128]{1,0:T(8,128)S(1)}, u32[]{:S(2)}, u32[]{:S(2)}) collective-permute-start(f32[36,128]{1,0:T(8,128)S(1)} %shard_map.114), channel_id=1, source_target_pairs={{0,2},{1,3},{2,0},{3,1},{4,6},{5,7},{6,4},{7,5},{8,10},{9,11},{10,... | collective-permute-start | bytes 55304 | tf_op jit(solution)/shard_map/ppermute | solution.py:343
  12.3 3.8 %collective-permute-start.1 = (f32[36,128]{1,0:T(8,128)S(1)}, f32[36,128]{1,0:T(8,128)S(1)}, u32[]{:S(2)}, u32[]{:S(2)}) collective-permute-start(f32[36,128]{1,0:T(8,128)S(1)} %shard_map.114), channel_id=1, source_target_pairs={{0,6},{1,7},{2,4},{3,5},{4,2},{5,3},{6,0},{7,1},{8,14},{9,15},{10,... | collective-permute-start | bytes 55304 | tf_op jit(solution)/shard_map/ppermute | solution.py:343
  12.3 3.8 %copy-start.1 = (f32[1,16,256]{2,1,0:T(8,128)S(1)}, f32[1,16,256]{2,1,0:T(8,128)}, u32[]{:S(2)}) copy-start(f32[1,16,256]{2,1,0:T(8,128)} %param.11) | copy-start | bytes 49156
  12.3 3.8 %copy-start.2 = (f32[1,16,256]{2,1,0:T(8,128)S(1)}, f32[1,16,256]{2,1,0:T(8,128)}, u32[]{:S(2)}) copy-start(f32[1,16,256]{2,1,0:T(8,128)} %param.12) | copy-start | bytes 49156

commit v4 on v3

--- a/solution.py
+++ b/solution.py
@@ -129,9 +129,16 @@
     lines_least(nodes_ref, lhs_ref, least_ref, None)
 
 
-def mate_kernel(mate_ref, nodes_ref, own_ref, least_ref, lhs_ref):
-    lhs_ref[...] = panel_terms(mate_ref[0:PAN, :])
-    lines_least(nodes_ref, lhs_ref, least_ref, own_ref)
+def mate_kernel(pay_ref, mate_ref, nodes_ref, own_ref, least_ref, lhs_ref):
+    lhs_ref[0:BLOCK, :] = panel_terms(mate_ref[0:PAN, :])
+    lhs_ref[BLOCK:, :] = panel_terms(pay_ref[0:PAN, :])
+    lines_least(nodes_ref, lhs_ref.at[0:BLOCK], least_ref, own_ref)
+    edge = [
+        jnp.concatenate([mate_ref[at : at + 1, :], mate_ref[at + 1 : at + 2, :]], axis=1)
+        for at in range(PAN + 6, PAN + EDGE, 2)
+    ]
+    best = line_least(edge, lhs_ref[...])
+    least_ref[LINES : LINES + 1, :] = jnp.min(best, axis=0, keepdims=True)
 
 
 def early_kernel(
@@ -242,8 +249,12 @@
         finish(i, best)
         return unused
 
-    for i in (0, 1 + LINES):
-        finish(i, jnp.min(line_least(coords(i), lhs_ref[...]), axis=0, keepdims=True))
+    inner = jnp.where(even, 1 + LINES, 0)
+    best = line_least(coords(inner), lhs_ref[0 : (PEERS - 2) * BLOCK, :])
+    best = jnp.minimum(jnp.min(best, axis=0, keepdims=True), done_ref[LINES : LINES + 1, :])
+    finish(inner, best)
+    outer = 1 + LINES - inner
+    finish(outer, jnp.min(line_least(coords(outer), lhs_ref[...]), axis=0, keepdims=True))
     lax.fori_loop(1, 1 + LINES, line, 0, unroll=UNROLL)
 
     mid_nu = sa_step(
@@ -284,11 +295,16 @@
     cells = got_ref[pl.ds(FR - 1, DEVS, stride=FR), :].T
     chosen = jnp.concatenate([cells[r * OB : (r + 1) * OB] for r in range(CAP)], axis=1)
     chosen = chosen.astype(BF16)
-    for v in range(VARS):
-        rows = jnp.concatenate(
+    def rows_of(v):
+        return jnp.concatenate(
             [got_ref[pl.ds(r * VARS + v, DEVS, stride=FR), :] for r in range(CAP)], axis=0
         )
-        out_ref[v] = add_up(chosen, rows)
+
+    for v in range(0, VARS, 2):
+        both = range(v, min(v + 2, VARS))
+        sums = add_up(chosen, jnp.concatenate([rows_of(w) for w in both], axis=1))
+        for n, w in enumerate(both):
+            out_ref[w] = sums[:, n * BLOCK : (n + 1) * BLOCK]
 
 
 def call(kernel, outs, *args, scratch=(), alias=(), hbm=(), fetch=True):
@@ -345,7 +361,9 @@
     three = swap(6)
     two = swap(4)
     one = swap(2)
-    (done,) = call(mate_kernel, [line], mate, nodes, own, scratch=(block,))
+    (done,) = call(
+        mate_kernel, [(24, NJ)], pay, mate, nodes, own, scratch=(pltpu.VMEM((2 * BLOCK, BLOCK), BF16),)
+    )
     ext = pltpu.VMEM((24, NJ), F32)
     dist, nu_next, send = call(
         step_kernel,

time: 50.1 us -> 49.9 us (level)
  transfers between devices with their start and end apart: 4 -> 4, of which waited for: 2 -> 2; matrix products, arithmetic and copies ran while one was open for 0% -> 0% of each run, Pallas kernels for 6% -> 7%
where the time goes in v4:
time: 49.9 us; the launch traced here: 49.7 us
  blocking collectives  24.1 us (48%)
  Pallas kernels  13.6 us (27%)
  starting transfers between devices  8.23 us (16%)
  waiting for transfers between devices  2.36 us (5%)
  between operations  0.73 us (1%)
  local copies, waits for them, and re-layouts  0.69 us (1%)
    all_to_all x1, blocking collectives, exchange(): lax.all_to_all(sent, axes, split_axis=0, concat_axis=0, tiled=True, axis_...  24.1 us
    pallas_call x6, Pallas kernels, call(): pl.pallas_call(kernel, out_shape=tuple(((jax.ShapeDtypeStruct if n in hbm...  13.6 us
    ppermute x3, starting transfers between devices, swap(): return lax.ppermute(near, 'blk', [(i, i ^ mask) for i in ring])  4.42 us
    ppermute x1, starting transfers between devices, per_device(): mate = lax.ppermute(pay, 'blk', [(i, i ^ 1) for i in ring])  3.81 us
    ppermute x3, waiting for transfers between devices, swap(): return lax.ppermute(near, 'blk', [(i, i ^ mask) for i in ring])  2.36 us
  transfers between devices with their start and end apart: 4, of which 2 were waited for; matrix products, arithmetic and copies ran while one was open for 0% of the time, Pallas kernels for 7%

profile of v4, /device:TPU:1, one launch (start us, length us, event | category | flops | bytes accessed | tf_op | source)
XLA Modules:
  0.0 49.7 jit_solution(1268252640545982021)
XLA Ops:
  0.6 0.0 copy-start.3
  0.6 0.0 copy-start
  0.6 0.9 %shard_map.112.pay_ref = f32[40,128]{1,0:T(8,128)S(1)} custom-call(f32[3,16,256]{2,1,0:T(8,128)} %bitcast.16, f32[3,1,512]{2,1,0:T(1,128)} %bitcast.25, f32[16,256]{1,0:T(8,128)} %bitcast.20, f32[16,256]{1,0:T(8,128)} %bitcast.22), custom_call_target="tpu_custom_call" | custom-call | tf_op jit(solution)/shard_map/pallas_call | solution.py:314
  1.5 0.0 copy-start.4
  1.6 3.8 %collective-permute-start = (f32[40,128]{1,0:T(8,128)S(1)}, f32[40,128]{1,0:T(8,128)S(1)}, u32[]{:S(2)}, u32[]{:S(2)}) collective-permute-start(f32[40,128]{1,0:T(8,128)S(1)} %shard_map.112.pay_ref), channel_id=1, source_target_pairs={{0,1},{1,0},{2,3},{3,2},{4,5},{5,4},{6,7},{7,6},{8,9},{9,8},{10,11... | collective-permute-start | bytes 61448 | tf_op jit(solution)/shard_map/ppermute | solution.py:340
  5.4 0.0 copy-done.3
  5.4 0.0 copy-done
  5.4 0.6 %copy-done.8 = s32[128]{0:T(128)S(1)} copy-done((s32[128]{0:T(128)S(1)}, s32[128]{0:T(128)}, u32[]{:S(2)}) %copy-start.8) | copy-done | bytes 536
  6.0 0.0 copy-done.5
  6.0 0.0 copy-done.6
  6.1 0.0 copy-done.7
  6.1 1.8 %shard_map.113 = (f32[16,256]{1,0:T(8,128)S(1)}, f32[1408,128]{1,0:T(8,128)S(1)}, f32[256,128]{1,0:T(8,128)S(1)}, f32[256,128]{1,0:T(8,128)S(1)}) custom-call(f32[3,1,512]{2,1,0:T(1,128)S(1)} %bitcast.26, f32[3,16,256]{2,1,0:T(8,128)S(1)} %bitcast.17, s32[1,128]{1,0:T(1,128)S(1)} %bitcast.27, s32[1,128]{1,0:T(1,128)S(1)} %bitcast.28, s32[1,128]{1,0:T(1,128)S(1)} %bitcast.29, ...), custom_call_target="tpu_custom_call" | custom-call | tf_op jit(solution)/shard_map/pallas_call | solution.py:314
  7.9 0.0 collective-permute-done.mate_ref
  7.9 3.7 %collective-permute-start.3 = (f32[36,128]{1,0:T(8,128)S(1)}, f32[36,128]{1,0:T(8,128)S(1)}, u32[]{:S(2)}, u32[]{:S(2)}) collective-permute-start(f32[36,128]{1,0:T(8,128)S(1)} %shard_map.114), channel_id=1, source_target_pairs={{0,4},{1,5},{2,6},{3,7},{4,0},{5,1},{6,2},{7,3},{8,12},{9,13},{10,... | collective-permute-start | bytes 55304 | tf_op jit(solution)/shard_map/ppermute | solution.py:359
  11.6 0.7 %collective-permute-start.2 = (f32[36,128]{1,0:T(8,128)S(1)}, f32[36,128]{1,0:T(8,128)S(1)}, u32[]{:S(2)}, u32[]{:S(2)}) collective-permute-start(f32[36,128]{1,0:T(8,128)S(1)} %shard_map.114), channel_id=1, source_target_pairs={{0,2},{1,3},{2,0},{3,1},{4,6},{5,7},{6,4},{7,5},{8,10},{9,11},{10,... | collective-permute-start | bytes 55304 | tf_op jit(solution)/shard_map/ppermute | solution.py:359
  12.3 0.0 collective-permute-start.1
  12.3 1.5 %shard_map.115.done_ref = f32[24,256]{1,0:T(8,128)S(1)} custom-call(f32[40,128]{1,0:T(8,128)S(1)} %shard_map.112.pay_ref, f32[40,128]{1,0:T(8,128)S(1)} %collective-permute-done.mate_ref, f32[3,16,256]{2,1,0:T(8,128)S(1)} %bitcast.18, f32[16,256]{1,0:T(8,128)S(1)} %get-tuple-element.10.least_ref.own_ref), custom_call_target="tpu_custom_call" | custom-call | tf_op jit(solution)/shard_map/pallas_call | solution.py:314
  13.8 0.0 collective-permute-done.3.two_ref
  13.8 0.4 collective-permute-done.2.one_ref
  14.2 1.9 %collective-permute-done.1.three_ref = f32[36,128]{1,0:T(8,128)S(1)} collective-permute-done((f32[36,128]{1,0:T(8,128)S(1)}, f32[36,128]{1,0:T(8,128)S(1)}, u32[]{:S(2)}, u32[]{:S(2)}) %collective-permute-start.1) | collective-permute-done | bytes 18464 | tf_op jit(solution)/shard_map/ppermute | solution.py:359
  16.1 0.0 copy-done.1
  16.2 8.6 %shard_map.116 = (f32[16,256]{1,0:T(8,128)}, f32[16,256]{1,0:T(8,128)}, f32[1408,128]{1,0:T(8,128)S(1)}) custom-call(f32[40,128]{1,0:T(8,128)S(1)} %shard_map.112.pay_ref, f32[40,128]{1,0:T(8,128)S(1)} %collective-permute-done.mate_ref, f32[36,128]{1,0:T(8,128)S(1)} %collective-permute-done.1.three_ref, ...), custom_call_target="tpu_custom_call", output_to_operand_aliasing={{2}: (11, {})} | custom-call | tf_op jit(solution)/shard_map/pallas_call | solution.py:314
  24.7 24.1 %all_to_all.5 = f32[128,1,1408]{2,1,0:T(1,128)S(1)} all-to-all(f32[128,1,1408]{2,1,0:T(1,128)S(1)} %bitcast.14), channel_id=1, replica_groups={{69,68,71,70,65,64,67,66,77,76,79,78,73,72,75,74,85,84,87,86,81,80,83,8..., dimensions={0} | all-to-all | bytes 1441792 | tf_op jit(solution)/shard_map/all_to_all | solution.py:329
  48.8 0.9 %shard_map.117 = f32[5,16,128]{2,1,0:T(8,128)} custom-call(f32[1408,128]{1,0:T(8,128)S(1)} %bitcast.15), custom_call_target="tpu_custom_call" | custom-call | tf_op jit(solution)/shard_map/pallas_call | solution.py:314
  (9 shorter events, 0.0 us)
Async XLA Ops:
  0.6 4.7 %copy-start.3 = (f32[1,4,16,256]{3,2,1,0:T(8,128)S(1)}, f32[1,4,16,256]{3,2,1,0:T(8,128)}, u32[]{:S(2)}) copy-start(f32[1,4,16,256]{3,2,1,0:T(8,128)} %param.13) | copy-start | bytes 196612
  0.6 4.7 %copy-start = (f32[1,3,16,256]{3,2,1,0:T(8,128)S(1)}, f32[1,3,16,256]{3,2,1,0:T(8,128)}, u32[]{:S(2)}) copy-start(f32[1,3,16,256]{3,2,1,0:T(8,128)} %param.9) | copy-start | bytes 147460
  1.5 3.9 %copy-start.4 = (f32[1,3,512]{2,0,1:T(1,128)S(1)}, f32[1,3,512]{2,0,1:T(1,128)}, u32[]{:S(2)}) copy-start(f32[1,3,512]{2,0,1:T(1,128)} %param.10) | copy-start | bytes 18436
  1.6 6.3 %collective-permute-start = (f32[40,128]{1,0:T(8,128)S(1)}, f32[40,128]{1,0:T(8,128)S(1)}, u32[]{:S(2)}, u32[]{:S(2)}) collective-permute-start(f32[40,128]{1,0:T(8,128)S(1)} %shard_map.112.pay_ref), channel_id=1, source_target_pairs={{0,1},{1,0},{2,3},{3,2},{4,5},{5,4},{6,7},{7,6},{8,9},{9,8},{10,11... | collective-permute-start | bytes 61448 | tf_op jit(solution)/shard_map/ppermute | solution.py:340
  5.4 0.7 %copy-start.8 = (s32[128]{0:T(128)S(1)}, s32[128]{0:T(128)}, u32[]{:S(2)}) copy-start(s32[128]{0:T(128)} %param.17) | copy-start | bytes 1540
  5.4 0.7 %copy-start.5 = (s32[128,1]{0,1:T(1,128)S(1)}, s32[128,1]{0,1:T(1,128)}, u32[]{:S(2)}) copy-start(s32[128,1]{0,1:T(1,128)} %param.16) | copy-start | bytes 1540
  5.4 0.7 %copy-start.6 = (s32[128]{0:T(128)S(1)}, s32[128]{0:T(128)}, u32[]{:S(2)}) copy-start(s32[128]{0:T(128)} %param.14) | copy-start | bytes 1540
  5.4 0.7 %copy-start.7 = (s32[128]{0:T(128)S(1)}, s32[128]{0:T(128)}, u32[]{:S(2)}) copy-start(s32[128]{0:T(128)} %param.15) | copy-start | bytes 1540
  7.9 5.9 %collective-permute-start.3 = (f32[36,128]{1,0:T(8,128)S(1)}, f32[36,128]{1,0:T(8,128)S(1)}, u32[]{:S(2)}, u32[]{:S(2)}) collective-permute-start(f32[36,128]{1,0:T(8,128)S(1)} %shard_map.114), channel_id=1, source_target_pairs={{0,4},{1,5},{2,6},{3,7},{4,0},{5,1},{6,2},{7,3},{8,12},{9,13},{10,... | collective-permute-start | bytes 55304 | tf_op jit(solution)/shard_map/ppermute | solution.py:359
  11.6 2.6 %collective-permute-start.2 = (f32[36,128]{1,0:T(8,128)S(1)}, f32[36,128]{1,0:T(8,128)S(1)}, u32[]{:S(2)}, u32[]{:S(2)}) collective-permute-start(f32[36,128]{1,0:T(8,128)S(1)} %shard_map.114), channel_id=1, source_target_pairs={{0,2},{1,3},{2,0},{3,1},{4,6},{5,7},{6,4},{7,5},{8,10},{9,11},{10,... | collective-permute-start | bytes 55304 | tf_op jit(solution)/shard_map/ppermute | solution.py:359
  12.3 3.8 %collective-permute-start.1 = (f32[36,128]{1,0:T(8,128)S(1)}, f32[36,128]{1,0:T(8,128)S(1)}, u32[]{:S(2)}, u32[]{:S(2)}) collective-permute-start(f32[36,128]{1,0:T(8,128)S(1)} %shard_map.114), channel_id=1, source_target_pairs={{0,6},{1,7},{2,4},{3,5},{4,2},{5,3},{6,0},{7,1},{8,14},{9,15},{10,... | collective-permute-start | bytes 55304 | tf_op jit(solution)/shard_map/ppermute | solution.py:359
  12.3 3.8 %copy-start.1 = (f32[1,16,256]{2,1,0:T(8,128)S(1)}, f32[1,16,256]{2,1,0:T(8,128)}, u32[]{:S(2)}) copy-start(f32[1,16,256]{2,1,0:T(8,128)} %param.11) | copy-start | bytes 49156
  12.3 3.8 %copy-start.2 = (f32[1,16,256]{2,1,0:T(8,128)S(1)}, f32[1,16,256]{2,1,0:T(8,128)}, u32[]{:S(2)}) copy-start(f32[1,16,256]{2,1,0:T(8,128)} %param.12) | copy-start | bytes 49156

commit v5 on v4

--- a/solution.py
+++ b/solution.py
@@ -200,7 +200,7 @@
 
 
 def step_kernel(
-    pay_ref, mate_ref, three_ref, one_ref, two_ref, done_ref, nodes_ref, nu_ref, vort_ref, pick_ref, live_ref, rows_ref,
+    pair_ref, mate_ref, three_ref, one_ref, two_ref, done_ref, nodes_ref, nu_ref, vort_ref, pick_ref, live_ref, rows_ref,
     dist_ref, next_ref, send_ref,
     lhs_ref, node_ext, nu_ext, vort_ext, dist_ext,
 ):
@@ -231,7 +231,6 @@
     vort_ext[1 + LINES : 2 + LINES, :] = edge(False, 4)
 
     sources = [(ref, at) for ref in (one_ref, two_ref, three_ref) for at in (0, PAN)]
-    sources += [(pay_ref, 0), (mate_ref, 0)]
     for k, (ref, at) in enumerate(sources):
         lhs_ref[k * BLOCK : (k + 1) * BLOCK, :] = panel_terms(ref[at : at + PAN, :])
 
@@ -244,17 +243,18 @@
         return [node_ext[c, pl.ds(i, 1), :] for c in range(3)]
 
     def line(i, unused):
-        best = line_least(coords(i), lhs_ref[0 : (PEERS - 2) * BLOCK, :])
+        best = line_least(coords(i), lhs_ref[...])
         best = jnp.minimum(jnp.min(best, axis=0, keepdims=True), done_ref[pl.ds(i - 1, 1), :])
         finish(i, best)
         return unused
 
     inner = jnp.where(even, 1 + LINES, 0)
-    best = line_least(coords(inner), lhs_ref[0 : (PEERS - 2) * BLOCK, :])
+    best = line_least(coords(inner), lhs_ref[...])
     best = jnp.minimum(jnp.min(best, axis=0, keepdims=True), done_ref[LINES : LINES + 1, :])
     finish(inner, best)
     outer = 1 + LINES - inner
-    finish(outer, jnp.min(line_least(coords(outer), lhs_ref[...]), axis=0, keepdims=True))
+    best = jnp.minimum(line_least(coords(outer), lhs_ref[...]), line_least(coords(outer), pair_ref[...]))
+    finish(outer, jnp.min(best, axis=0, keepdims=True))
     lax.fori_loop(1, 1 + LINES, line, 0, unroll=UNROLL)
 
     mid_nu = sa_step(
@@ -307,14 +307,14 @@
             out_ref[w] = sums[:, n * BLOCK : (n + 1) * BLOCK]
 
 
-def call(kernel, outs, *args, scratch=(), alias=(), hbm=(), fetch=True):
+def call(kernel, outs, *args, scratch=(), alias=(), hbm=(), fetch=True, types=()):
     if fetch:
         args = [pltpu.with_memory_space_constraint(a, pltpu.VMEM) for a in args]
     vmem = pl.BlockSpec(memory_space=pltpu.VMEM)
     return pl.pallas_call(
         kernel,
         out_shape=tuple(
-            (jax.ShapeDtypeStruct if n in hbm else pltpu.VMEM)(shape, F32)
+            (jax.ShapeDtypeStruct if n in hbm else pltpu.VMEM)(shape, dict(types).get(n, F32))
             for n, shape in enumerate(outs)
         ),
         in_specs=[vmem] * len(args),
@@ -361,16 +361,19 @@
     three = swap(6)
     two = swap(4)
     one = swap(2)
-    (done,) = call(
-        mate_kernel, [(24, NJ)], pay, mate, nodes, own, scratch=(pltpu.VMEM((2 * BLOCK, BLOCK), BF16),)
+    done, pair_terms = call(
+        mate_kernel,
+        [(24, NJ), (2 * BLOCK, BLOCK)],
+        pay, mate, nodes, own,
+        types=((1, BF16),),
     )
     ext = pltpu.VMEM((24, NJ), F32)
     dist, nu_next, send = call(
         step_kernel,
         [line, line, (DEVS * FR, BLOCK)],
-        pay, mate, three, one, two, done, nodes, nu, vort, pick, live, send,
+        pair_terms, mate, three, one, two, done, nodes, nu, vort, pick, live, send,
         scratch=(
-            pltpu.VMEM((PEERS * BLOCK, BLOCK), BF16),
+            pltpu.VMEM(((PEERS - 2) * BLOCK, BLOCK), BF16),
             pltpu.VMEM((3, 24, NJ), F32),
             ext, ext, ext,
         ),

time: 49.9 us -> 49.9 us (level)
  no operation moved by 1% of the time
where the time goes in v5:
time: 49.9 us; the launch traced here: 49.7 us
  blocking collectives  24.1 us (48%)
  Pallas kernels  13.6 us (27%)
  starting transfers between devices  8.23 us (16%)
  waiting for transfers between devices  2.36 us (5%)
  between operations  0.73 us (1%)
  local copies, waits for them, and re-layouts  0.69 us (1%)
    all_to_all x1, blocking collectives, exchange(): lax.all_to_all(sent, axes, split_axis=0, concat_axis=0, tiled=True, axis_...  24.1 us
    pallas_call x6, Pallas kernels, call(): pl.pallas_call(kernel, out_shape=tuple(((jax.ShapeDtypeStruct if n in hbm...  13.6 us
    ppermute x3, starting transfers between devices, swap(): return lax.ppermute(near, 'blk', [(i, i ^ mask) for i in ring])  4.42 us
    ppermute x1, starting transfers between devices, per_device(): mate = lax.ppermute(pay, 'blk', [(i, i ^ 1) for i in ring])  3.81 us
    ppermute x3, waiting for transfers between devices, swap(): return lax.ppermute(near, 'blk', [(i, i ^ mask) for i in ring])  2.36 us
  transfers between devices with their start and end apart: 4, of which 2 were waited for; matrix products, arithmetic and copies ran while one was open for 0% of the time, Pallas kernels for 7%

profile of v5, /device:TPU:1, one launch (start us, length us, event | category | flops | bytes accessed | tf_op | source)
XLA Modules:
  0.0 49.7 jit_solution(4921312915254350368)
XLA Ops:
  0.6 0.0 copy-start.3
  0.6 0.0 copy-start
  0.6 0.9 %shard_map.112.pay_ref = f32[40,128]{1,0:T(8,128)S(1)} custom-call(f32[3,16,256]{2,1,0:T(8,128)} %bitcast.16, f32[3,1,512]{2,1,0:T(1,128)} %bitcast.25, f32[16,256]{1,0:T(8,128)} %bitcast.20, f32[16,256]{1,0:T(8,128)} %bitcast.22), custom_call_target="tpu_custom_call" | custom-call | tf_op jit(solution)/shard_map/pallas_call | solution.py:314
  1.5 0.0 copy-start.4
  1.6 3.8 %collective-permute-start = (f32[40,128]{1,0:T(8,128)S(1)}, f32[40,128]{1,0:T(8,128)S(1)}, u32[]{:S(2)}, u32[]{:S(2)}) collective-permute-start(f32[40,128]{1,0:T(8,128)S(1)} %shard_map.112.pay_ref), channel_id=1, source_target_pairs={{0,1},{1,0},{2,3},{3,2},{4,5},{5,4},{6,7},{7,6},{8,9},{9,8},{10,11... | collective-permute-start | bytes 61448 | tf_op jit(solution)/shard_map/ppermute | solution.py:340
  5.4 0.0 copy-done.3
  5.4 0.0 copy-done
  5.4 0.6 %copy-done.8 = s32[128]{0:T(128)S(1)} copy-done((s32[128]{0:T(128)S(1)}, s32[128]{0:T(128)}, u32[]{:S(2)}) %copy-start.8) | copy-done | bytes 536
  6.0 0.0 copy-done.5
  6.0 0.0 copy-done.6
  6.1 0.0 copy-done.7
  6.1 1.8 %shard_map.113 = (f32[16,256]{1,0:T(8,128)S(1)}, f32[1408,128]{1,0:T(8,128)S(1)}, f32[256,128]{1,0:T(8,128)S(1)}, f32[256,128]{1,0:T(8,128)S(1)}) custom-call(f32[3,1,512]{2,1,0:T(1,128)S(1)} %bitcast.26, f32[3,16,256]{2,1,0:T(8,128)S(1)} %bitcast.17, s32[1,128]{1,0:T(1,128)S(1)} %bitcast.27, s32[1,128]{1,0:T(1,128)S(1)} %bitcast.28, s32[1,128]{1,0:T(1,128)S(1)} %bitcast.29, ...), custom_call_target="tpu_custom_call" | custom-call | tf_op jit(solution)/shard_map/pallas_call | solution.py:314
  7.9 0.0 collective-permute-done.mate_ref
  7.9 3.7 %collective-permute-start.3 = (f32[36,128]{1,0:T(8,128)S(1)}, f32[36,128]{1,0:T(8,128)S(1)}, u32[]{:S(2)}, u32[]{:S(2)}) collective-permute-start(f32[36,128]{1,0:T(8,128)S(1)} %shard_map.115), channel_id=1, source_target_pairs={{0,4},{1,5},{2,6},{3,7},{4,0},{5,1},{6,2},{7,3},{8,12},{9,13},{10,... | collective-permute-start | bytes 55304 | tf_op jit(solution)/shard_map/ppermute | solution.py:359
  11.6 0.7 %collective-permute-start.2 = (f32[36,128]{1,0:T(8,128)S(1)}, f32[36,128]{1,0:T(8,128)S(1)}, u32[]{:S(2)}, u32[]{:S(2)}) collective-permute-start(f32[36,128]{1,0:T(8,128)S(1)} %shard_map.115), channel_id=1, source_target_pairs={{0,2},{1,3},{2,0},{3,1},{4,6},{5,7},{6,4},{7,5},{8,10},{9,11},{10,... | collective-permute-start | bytes 55304 | tf_op jit(solution)/shard_map/ppermute | solution.py:359
  12.3 0.0 collective-permute-start.1
  12.3 1.5 %shard_map.114 = (f32[24,256]{1,0:T(8,128)S(1)}, bf16[256,128]{1,0:T(8,128)(2,1)S(1)}) custom-call(f32[40,128]{1,0:T(8,128)S(1)} %shard_map.112.pay_ref, f32[40,128]{1,0:T(8,128)S(1)} %collective-permute-done.mate_ref, f32[3,16,256]{2,1,0:T(8,128)S(1)} %bitcast.18, f32[16,256]{1,0:T(8,128)S(1)} %get-tuple-element.12.own_ref.least_ref), custom_call_target="tpu_custom_call" | custom-call | tf_op jit(solution)/shard_map/pallas_call | solution.py:314
  13.8 0.0 collective-permute-done.3.two_ref
  13.8 0.4 collective-permute-done.2.one_ref
  14.2 1.9 %collective-permute-done.1.three_ref = f32[36,128]{1,0:T(8,128)S(1)} collective-permute-done((f32[36,128]{1,0:T(8,128)S(1)}, f32[36,128]{1,0:T(8,128)S(1)}, u32[]{:S(2)}, u32[]{:S(2)}) %collective-permute-start.1) | collective-permute-done | bytes 18464 | tf_op jit(solution)/shard_map/ppermute | solution.py:359
  16.1 0.0 copy-done.1
  16.2 8.6 %shard_map.116 = (f32[16,256]{1,0:T(8,128)}, f32[16,256]{1,0:T(8,128)}, f32[1408,128]{1,0:T(8,128)S(1)}) custom-call(bf16[256,128]{1,0:T(8,128)(2,1)S(1)} %get-tuple-element.13.pair_ref, f32[40,128]{1,0:T(8,128)S(1)} %collective-permute-done.mate_ref, f32[36,128]{1,0:T(8,128)S(1)} %collective-permute-done.1.three_ref, ...), custom_call_target="tpu_custom_call", output_to_operand_aliasing={{2}: (11, {})} | custom-call | tf_op jit(solution)/shard_map/pallas_call | solution.py:314
  24.7 24.1 %all_to_all.5 = f32[128,1,1408]{2,1,0:T(1,128)S(1)} all-to-all(f32[128,1,1408]{2,1,0:T(1,128)S(1)} %bitcast.14), channel_id=1, replica_groups={{69,68,71,70,65,64,67,66,77,76,79,78,73,72,75,74,85,84,87,86,81,80,83,8..., dimensions={0} | all-to-all | bytes 1441792 | tf_op jit(solution)/shard_map/all_to_all | solution.py:329
  48.8 0.9 %shard_map.117 = f32[5,16,128]{2,1,0:T(8,128)} custom-call(f32[1408,128]{1,0:T(8,128)S(1)} %bitcast.15), custom_call_target="tpu_custom_call" | custom-call | tf_op jit(solution)/shard_map/pallas_call | solution.py:314
  (9 shorter events, 0.0 us)
Async XLA Ops:
  0.6 4.7 %copy-start.3 = (f32[1,4,16,256]{3,2,1,0:T(8,128)S(1)}, f32[1,4,16,256]{3,2,1,0:T(8,128)}, u32[]{:S(2)}) copy-start(f32[1,4,16,256]{3,2,1,0:T(8,128)} %param.13) | copy-start | bytes 196612
  0.6 4.7 %copy-start = (f32[1,3,16,256]{3,2,1,0:T(8,128)S(1)}, f32[1,3,16,256]{3,2,1,0:T(8,128)}, u32[]{:S(2)}) copy-start(f32[1,3,16,256]{3,2,1,0:T(8,128)} %param.9) | copy-start | bytes 147460
  1.5 3.9 %copy-start.4 = (f32[1,3,512]{2,0,1:T(1,128)S(1)}, f32[1,3,512]{2,0,1:T(1,128)}, u32[]{:S(2)}) copy-start(f32[1,3,512]{2,0,1:T(1,128)} %param.10) | copy-start | bytes 18436
  1.6 6.3 %collective-permute-start = (f32[40,128]{1,0:T(8,128)S(1)}, f32[40,128]{1,0:T(8,128)S(1)}, u32[]{:S(2)}, u32[]{:S(2)}) collective-permute-start(f32[40,128]{1,0:T(8,128)S(1)} %shard_map.112.pay_ref), channel_id=1, source_target_pairs={{0,1},{1,0},{2,3},{3,2},{4,5},{5,4},{6,7},{7,6},{8,9},{9,8},{10,11... | collective-permute-start | bytes 61448 | tf_op jit(solution)/shard_map/ppermute | solution.py:340
  5.4 0.7 %copy-start.8 = (s32[128]{0:T(128)S(1)}, s32[128]{0:T(128)}, u32[]{:S(2)}) copy-start(s32[128]{0:T(128)} %param.17) | copy-start | bytes 1540
  5.4 0.7 %copy-start.5 = (s32[128,1]{0,1:T(1,128)S(1)}, s32[128,1]{0,1:T(1,128)}, u32[]{:S(2)}) copy-start(s32[128,1]{0,1:T(1,128)} %param.16) | copy-start | bytes 1540
  5.4 0.7 %copy-start.6 = (s32[128]{0:T(128)S(1)}, s32[128]{0:T(128)}, u32[]{:S(2)}) copy-start(s32[128]{0:T(128)} %param.14) | copy-start | bytes 1540
  5.4 0.7 %copy-start.7 = (s32[128]{0:T(128)S(1)}, s32[128]{0:T(128)}, u32[]{:S(2)}) copy-start(s32[128]{0:T(128)} %param.15) | copy-start | bytes 1540
  7.9 5.9 %collective-permute-start.3 = (f32[36,128]{1,0:T(8,128)S(1)}, f32[36,128]{1,0:T(8,128)S(1)}, u32[]{:S(2)}, u32[]{:S(2)}) collective-permute-start(f32[36,128]{1,0:T(8,128)S(1)} %shard_map.115), channel_id=1, source_target_pairs={{0,4},{1,5},{2,6},{3,7},{4,0},{5,1},{6,2},{7,3},{8,12},{9,13},{10,... | collective-permute-start | bytes 55304 | tf_op jit(solution)/shard_map/ppermute | solution.py:359
  11.6 2.6 %collective-permute-start.2 = (f32[36,128]{1,0:T(8,128)S(1)}, f32[36,128]{1,0:T(8,128)S(1)}, u32[]{:S(2)}, u32[]{:S(2)}) collective-permute-start(f32[36,128]{1,0:T(8,128)S(1)} %shard_map.115), channel_id=1, source_target_pairs={{0,2},{1,3},{2,0},{3,1},{4,6},{5,7},{6,4},{7,5},{8,10},{9,11},{10,... | collective-permute-start | bytes 55304 | tf_op jit(solution)/shard_map/ppermute | solution.py:359
  12.3 3.8 %collective-permute-start.1 = (f32[36,128]{1,0:T(8,128)S(1)}, f32[36,128]{1,0:T(8,128)S(1)}, u32[]{:S(2)}, u32[]{:S(2)}) collective-permute-start(f32[36,128]{1,0:T(8,128)S(1)} %shard_map.115), channel_id=1, source_target_pairs={{0,6},{1,7},{2,4},{3,5},{4,2},{5,3},{6,0},{7,1},{8,14},{9,15},{10,... | collective-permute-start | bytes 55304 | tf_op jit(solution)/shard_map/ppermute | solution.py:359
  12.3 3.8 %copy-start.1 = (f32[1,16,256]{2,1,0:T(8,128)S(1)}, f32[1,16,256]{2,1,0:T(8,128)}, u32[]{:S(2)}) copy-start(f32[1,16,256]{2,1,0:T(8,128)} %param.11) | copy-start | bytes 49156
  12.3 3.8 %copy-start.2 = (f32[1,16,256]{2,1,0:T(8,128)S(1)}, f32[1,16,256]{2,1,0:T(8,128)}, u32[]{:S(2)}) copy-start(f32[1,16,256]{2,1,0:T(8,128)} %param.12) | copy-start | bytes 49156
